TPU v7x, 128 devices: a whole 4x4x4 slice. The times are simulated.
128 devices in a mesh: sensor: 8 (over x, z_lo), chan: 16 (over z_hi, y, core).
Axes of the slice: x: 4, y: 4, z: 4 (z_hi: 2, z_lo: 2; z = z_hi * 2 + z_lo), core: 2. Of those that a mesh axis runs over, the one named last changes fastest.
Arguments:
- samples: float32 [2, 128, 512, 128], P(None, 'sensor', 'chan'), may hold values from -6 to 6
- bins: int32 [64], replicated, may hold values from 1 to 511
- offsets: int32 [64], replicated, may hold values from 0 to 7
Outputs:
- gram: float32 [64, 2, 128, 128], P('chan', None, 'sensor')
All inputs are finite; a program needn't handle non-finite values.
Results may differ from a plain program's by a relative error of at most 0.00009.
Values sent between devices are 32-bit elements; how exact they have to be, the bound alone decides.
A program may use at most 64 MiB of HBM per device.

v0:
```python
import math

import jax
import jax.numpy as jnp
from jax import lax
from jax.sharding import Mesh
from jax.sharding import PartitionSpec as P

SENSOR = ("sensor_0", "sensor_1")


power_floor = 0.1


def shifted_2(block, axis, distance):
    devices = range(lax.axis_size(axis))
    route = [((i - distance) % len(devices), i) for i in devices]
    return lax.ppermute(block, axis, route)


def whole_of(x, axes, dim):
    for axis in reversed(axes):
        x = lax.all_gather(x, axis, axis=dim, tiled=True)
    return x


def in_blocks(x, dim, count):
    before, after = (x.shape[:dim], x.shape[dim + 1 :])
    return jnp.moveaxis(x.reshape(*before, count, -1, *after), dim, 0)


def sent_and_summed(x, axis, dim):
    count = lax.axis_size(axis)
    tiles = lax.all_to_all(in_blocks(x, dim, count), axis, 0, 0, tiled=True)
    return jnp.sum(tiles, axis=0)


def dft_table(length):
    indices = jnp.arange(length, dtype=jnp.int32)
    phases = indices[:, None] * indices[None, :] % length
    angles = phases.astype(jnp.float32) * (2.0 * math.pi / length)
    cosine = jnp.cos(angles) / math.sqrt(length)
    sine_part = jnp.sin(angles) / math.sqrt(length)
    upper = jnp.concatenate([cosine, -sine_part], 1)
    bottom = jnp.concatenate([sine_part, cosine], 1)
    return jnp.concatenate([upper, bottom], 0)


def gram_columns(extended, rim_len, bins, offsets, columns, factor):
    column_count = columns.shape[3]
    sensors_here = extended.shape[3]
    chans = extended.shape[0] - rim_len
    length = extended.shape[1] // 2
    flattened = columns.reshape(chans * length, 2 * column_count)

    def one_alpha(cycle_bin, offset):
        start = rim_len - offset
        shifted = lax.dynamic_slice(
            extended,
            (start, cycle_bin, jnp.int32(0), jnp.int32(0)),
            (chans, length, 2, sensors_here),
        )
        return shifted.reshape(chans * length, 2 * sensors_here)

    def one_block(inputs_pair):
        cycle_bins, channel_shifts = inputs_pair
        left_rows = jax.vmap(one_alpha)(cycle_bins, channel_shifts)
        cross = jnp.einsum("akp,kq->apq", left_rows, flattened, precision=lax.Precision.HIGHEST)
        cross = cross.reshape(cross.shape[0], 2, sensors_here, 2, column_count)
        real_sum = cross[:, 0, :, 0] + cross[:, 1, :, 1]
        imag_sum = cross[:, 1, :, 0] - cross[:, 0, :, 1]
        return jnp.stack([real_sum, imag_sum], 1)

    blocks_out = lax.map(one_block, (bins.reshape(-1, 4), offsets.reshape(-1, 4)))
    return blocks_out.reshape(-1, 2, sensors_here, column_count) * factor


def on_device(samples, bins, offsets):
    chan_count = lax.axis_size("chan")
    sensors_here = samples.shape[1]
    blocks_here = samples.shape[2]
    channel_count = samples.shape[3]
    positions = jnp.arange(channel_count, dtype=jnp.float32)
    window = 0.5 - 0.5 * jnp.cos(positions * (2.0 * math.pi / channel_count))
    framed = jnp.concatenate([samples[0] * window, samples[1] * window], 2)
    demodulates = jnp.einsum(
        "sbn,nk->skb", framed, dft_table(channel_count), precision=lax.Precision.HIGHEST
    )
    demodulates = demodulates.reshape(sensors_here, 2, channel_count, blocks_here)
    received = lax.all_to_all(demodulates, "chan", split_axis=2, concat_axis=3, tiled=True)
    length = received.shape[3]
    joined = jnp.concatenate([received[:, 0], received[:, 1]], 2)
    transformed = jnp.einsum(
        "ncf,fg->ncg", joined, dft_table(length), precision=lax.Precision.HIGHEST
    )
    real_part = transformed[..., :length]
    imag_part = transformed[..., length:]
    scaling = 1.0 / jnp.sqrt(real_part * real_part + imag_part * imag_part + power_floor)
    spectra = jnp.stack([real_part * scaling, imag_part * scaling], 1)
    spectra = jnp.transpose(spectra, (2, 3, 1, 0))
    chans = spectra.shape[0]
    length = spectra.shape[1]
    lower_rim = shifted_2(spectra[1:], "chan", 1)
    rim_len = lower_rim.shape[0]
    extended = jnp.concatenate([lower_rim, spectra], 0)
    extended = jnp.concatenate([extended, extended], 1)
    factor = 1.0 / math.sqrt(chans * chan_count * length)
    everyone = whole_of(spectra, SENSOR, 3)
    partial_value = gram_columns(extended, rim_len, bins, offsets, everyone, factor)
    return sent_and_summed(partial_value, "chan", 0)


def solution(mesh):
    finer = Mesh(mesh.devices.reshape(4, 2, mesh.shape["chan"]), ("sensor_0", "sensor_1", "chan"))
    return jax.shard_map(
        on_device,
        mesh=finer,
        in_specs=(P(None, SENSOR, "chan", None), P(), P()),
        out_specs=P("chan", None, SENSOR, None),
        check_vma=False,
    )
```

profile of v0, /device:TPU:1, one launch (start us, length us, event | category | flops | bytes accessed | tf_op | source)
XLA Modules:
  0.0 552.2 jit_solution(16591768203287099731)
XLA Ops:
  11.0 2.8 reshape.188
  13.9 9.3 %all-to-all-start = ((f32[16,1,8192]{2,1,0:T(1,128)}), f32[16,1,8192]{2,1,0:T(1,128)S(1)}, u32[]{:S(2)}, u32[]{:S(2)}) async-start(f32[16,1,8192]{2,1,0:T(1,128)} %reshape.188), calls=%async_computation | async-start | bytes 1048576 | tf_op jit(solution)/shard_map/all_to_all | solution.py:90
  23.4 4.7 fusion.24
  28.0 5.0 sine_multiply_fusion
  41.2 4.6 fusion.5
  46.8 23.7 %all-gather.3.cloned.1.call-done = f32[8,512,2,32]{1,0,3,2:T(8,128)} async-done(((f32[8,512,2,16]{1,0,3,2:T(8,128)}), f32[8,512,2,32]{1,0,3,2:T(8,128)}) %all-gather.3.cloned.1.call-update) | async-done | bytes 1048592 | tf_op jit(solution)/shard_map/all_gather | solution.py:23
  73.9 6.0 %collective-permute-done = f32[7,512,2,16]{1,0,3,2:T(8,128)S(1)} collective-permute-done((f32[7,512,2,16]{1,0,3,2:T(8,128)S(1)}, f32[7,512,2,16]{1,0,3,2:T(8,128)S(1)}, u32[]{:S(2)}, u32[]{:S(2)}) %collective-permute-start) | collective-permute-done | bytes 458784 | tf_op jit(solution)/shard_map/ppermute | solution.py:18
  82.7 38.7 %all-gather.5.cloned.1.call-done = f32[8,512,2,128]{1,0,3,2:T(8,128)} async-done(((f32[8,512,2,32]{1,0,3,2:T(8,128)}), f32[8,512,2,128]{1,0,3,2:T(8,128)}) %all-gather.5.cloned.1.call-update) | async-done | bytes 4194320 | tf_op jit(solution)/shard_map/all_gather | solution.py:23
  121.4 7.9 %copy.34 = f32[32,8,8,512]{3,1,2,0:T(8,128)} copy(f32[32,8,8,512]{3,2,1,0:T(8,128)} %bitcast.122) | data formatting | bytes 8388608
  129.3 390.9 %while.15 = (s32[]{:T(128)}, f32[16,4,2,16,128]{4,3,1,2,0:T(8,128)S(1)}, s32[16,4]{1,0:T(8,128)S(1)}, s32[16,4]{1,0:T(8,128)S(1)}, f32[15,1024,2,16]{1,3,2,0:T(8...) while((s32[]{:T(128)}, f32[16,4,2,16,128]{4,3,1,2,0:T(8,128)S(1)}, ...), condition=%wide.region_1.2_spmd, body=%wide.region_0.1_spmd.sunk | while | flops 1610645504 | bytes 13042726 | solution.py:74
  129.7 17.0 %while.16 = (s32[]{:T(128)}, f32[15,1024,2,16]{1,3,2,0:T(8,128)}, s32[4,4]{1,0:T(4,128)S(1)}, f32[4,8,512,2,16]{2,1,4,3,0:T(8,128)}, s32[]{:T(128)}) while((s32[]{:T(128)}, f32[15,1024,2,16]{1,3,2,0:T(8,128)}, s32[4,4]{1,0:T(4,128)S(1)}, f32[4,8,512,2,16]{2,1,4,3,0:T(8,128)}, s32[]{:T(128)}) %tuple.55), condition=%wide.while_cond, body=%wide.while_body.sunk | while | flops 2 | bytes 2097785 | solution.py:58
  138.7 2.5 dynamic-slice_bitcast_fusion.2
  143.0 2.5 dynamic-slice_bitcast_fusion.2
  148.4 5.3 fusion.53
  154.1 17.0 %while.16 = (s32[]{:T(128)}, f32[15,1024,2,16]{1,3,2,0:T(8,128)}, s32[4,4]{1,0:T(4,128)S(1)}, f32[4,8,512,2,16]{2,1,4,3,0:T(8,128)}, s32[]{:T(128)}) while((s32[]{:T(128)}, f32[15,1024,2,16]{1,3,2,0:T(8,128)}, s32[4,4]{1,0:T(4,128)S(1)}, f32[4,8,512,2,16]{2,1,4,3,0:T(8,128)}, s32[]{:T(128)}) %tuple.55), condition=%wide.while_cond, body=%wide.while_body.sunk | while | flops 2 | bytes 2097785 | solution.py:58
  154.7 2.5 dynamic-slice_bitcast_fusion.2
  158.9 2.5 dynamic-slice_bitcast_fusion.2
  163.2 2.5 dynamic-slice_bitcast_fusion.2
  172.8 5.3 fusion.53
  178.5 17.0 %while.16 = (s32[]{:T(128)}, f32[15,1024,2,16]{1,3,2,0:T(8,128)}, s32[4,4]{1,0:T(4,128)S(1)}, f32[4,8,512,2,16]{2,1,4,3,0:T(8,128)}, s32[]{:T(128)}) while((s32[]{:T(128)}, f32[15,1024,2,16]{1,3,2,0:T(8,128)}, s32[4,4]{1,0:T(4,128)S(1)}, f32[4,8,512,2,16]{2,1,4,3,0:T(8,128)}, s32[]{:T(128)}) %tuple.55), condition=%wide.while_cond, body=%wide.while_body.sunk | while | flops 2 | bytes 2097785 | solution.py:58
  197.2 5.3 fusion.53
  203.0 17.0 %while.16 = (s32[]{:T(128)}, f32[15,1024,2,16]{1,3,2,0:T(8,128)}, s32[4,4]{1,0:T(4,128)S(1)}, f32[4,8,512,2,16]{2,1,4,3,0:T(8,128)}, s32[]{:T(128)}) while((s32[]{:T(128)}, f32[15,1024,2,16]{1,3,2,0:T(8,128)}, s32[4,4]{1,0:T(4,128)S(1)}, f32[4,8,512,2,16]{2,1,4,3,0:T(8,128)}, s32[]{:T(128)}) %tuple.55), condition=%wide.while_cond, body=%wide.while_body.sunk | while | flops 2 | bytes 2097785 | solution.py:58
  221.7 5.3 fusion.53
  227.4 17.0 %while.16 = (s32[]{:T(128)}, f32[15,1024,2,16]{1,3,2,0:T(8,128)}, s32[4,4]{1,0:T(4,128)S(1)}, f32[4,8,512,2,16]{2,1,4,3,0:T(8,128)}, s32[]{:T(128)}) while((s32[]{:T(128)}, f32[15,1024,2,16]{1,3,2,0:T(8,128)}, s32[4,4]{1,0:T(4,128)S(1)}, f32[4,8,512,2,16]{2,1,4,3,0:T(8,128)}, s32[]{:T(128)}) %tuple.55), condition=%wide.while_cond, body=%wide.while_body.sunk | while | flops 2 | bytes 2097785 | solution.py:58
  246.1 5.3 fusion.53
  251.8 17.0 %while.16 = (s32[]{:T(128)}, f32[15,1024,2,16]{1,3,2,0:T(8,128)}, s32[4,4]{1,0:T(4,128)S(1)}, f32[4,8,512,2,16]{2,1,4,3,0:T(8,128)}, s32[]{:T(128)}) while((s32[]{:T(128)}, f32[15,1024,2,16]{1,3,2,0:T(8,128)}, s32[4,4]{1,0:T(4,128)S(1)}, f32[4,8,512,2,16]{2,1,4,3,0:T(8,128)}, s32[]{:T(128)}) %tuple.55), condition=%wide.while_cond, body=%wide.while_body.sunk | while | flops 2 | bytes 2097785 | solution.py:58
  270.5 5.3 fusion.53
  276.3 17.0 %while.16 = (s32[]{:T(128)}, f32[15,1024,2,16]{1,3,2,0:T(8,128)}, s32[4,4]{1,0:T(4,128)S(1)}, f32[4,8,512,2,16]{2,1,4,3,0:T(8,128)}, s32[]{:T(128)}) while((s32[]{:T(128)}, f32[15,1024,2,16]{1,3,2,0:T(8,128)}, s32[4,4]{1,0:T(4,128)S(1)}, f32[4,8,512,2,16]{2,1,4,3,0:T(8,128)}, s32[]{:T(128)}) %tuple.55), condition=%wide.while_cond, body=%wide.while_body.sunk | while | flops 2 | bytes 2097785 | solution.py:58
  295.0 5.3 fusion.53
  300.7 17.0 %while.16 = (s32[]{:T(128)}, f32[15,1024,2,16]{1,3,2,0:T(8,128)}, s32[4,4]{1,0:T(4,128)S(1)}, f32[4,8,512,2,16]{2,1,4,3,0:T(8,128)}, s32[]{:T(128)}) while((s32[]{:T(128)}, f32[15,1024,2,16]{1,3,2,0:T(8,128)}, s32[4,4]{1,0:T(4,128)S(1)}, f32[4,8,512,2,16]{2,1,4,3,0:T(8,128)}, s32[]{:T(128)}) %tuple.55), condition=%wide.while_cond, body=%wide.while_body.sunk | while | flops 2 | bytes 2097785 | solution.py:58
  319.4 5.3 fusion.53
  325.1 17.0 %while.16 = (s32[]{:T(128)}, f32[15,1024,2,16]{1,3,2,0:T(8,128)}, s32[4,4]{1,0:T(4,128)S(1)}, f32[4,8,512,2,16]{2,1,4,3,0:T(8,128)}, s32[]{:T(128)}) while((s32[]{:T(128)}, f32[15,1024,2,16]{1,3,2,0:T(8,128)}, s32[4,4]{1,0:T(4,128)S(1)}, f32[4,8,512,2,16]{2,1,4,3,0:T(8,128)}, s32[]{:T(128)}) %tuple.55), condition=%wide.while_cond, body=%wide.while_body.sunk | while | flops 2 | bytes 2097785 | solution.py:58
  343.8 5.3 fusion.53
  349.5 17.0 %while.16 = (s32[]{:T(128)}, f32[15,1024,2,16]{1,3,2,0:T(8,128)}, s32[4,4]{1,0:T(4,128)S(1)}, f32[4,8,512,2,16]{2,1,4,3,0:T(8,128)}, s32[]{:T(128)}) while((s32[]{:T(128)}, f32[15,1024,2,16]{1,3,2,0:T(8,128)}, s32[4,4]{1,0:T(4,128)S(1)}, f32[4,8,512,2,16]{2,1,4,3,0:T(8,128)}, s32[]{:T(128)}) %tuple.55), condition=%wide.while_cond, body=%wide.while_body.sunk | while | flops 2 | bytes 2097785 | solution.py:58
  368.3 5.3 fusion.53
  374.0 17.0 %while.16 = (s32[]{:T(128)}, f32[15,1024,2,16]{1,3,2,0:T(8,128)}, s32[4,4]{1,0:T(4,128)S(1)}, f32[4,8,512,2,16]{2,1,4,3,0:T(8,128)}, s32[]{:T(128)}) while((s32[]{:T(128)}, f32[15,1024,2,16]{1,3,2,0:T(8,128)}, s32[4,4]{1,0:T(4,128)S(1)}, f32[4,8,512,2,16]{2,1,4,3,0:T(8,128)}, s32[]{:T(128)}) %tuple.55), condition=%wide.while_cond, body=%wide.while_body.sunk | while | flops 2 | bytes 2097785 | solution.py:58
  392.7 5.3 fusion.53
  398.4 17.0 %while.16 = (s32[]{:T(128)}, f32[15,1024,2,16]{1,3,2,0:T(8,128)}, s32[4,4]{1,0:T(4,128)S(1)}, f32[4,8,512,2,16]{2,1,4,3,0:T(8,128)}, s32[]{:T(128)}) while((s32[]{:T(128)}, f32[15,1024,2,16]{1,3,2,0:T(8,128)}, s32[4,4]{1,0:T(4,128)S(1)}, f32[4,8,512,2,16]{2,1,4,3,0:T(8,128)}, s32[]{:T(128)}) %tuple.55), condition=%wide.while_cond, body=%wide.while_body.sunk | while | flops 2 | bytes 2097785 | solution.py:58
  417.1 5.3 fusion.53
  422.8 17.0 %while.16 = (s32[]{:T(128)}, f32[15,1024,2,16]{1,3,2,0:T(8,128)}, s32[4,4]{1,0:T(4,128)S(1)}, f32[4,8,512,2,16]{2,1,4,3,0:T(8,128)}, s32[]{:T(128)}) while((s32[]{:T(128)}, f32[15,1024,2,16]{1,3,2,0:T(8,128)}, s32[4,4]{1,0:T(4,128)S(1)}, f32[4,8,512,2,16]{2,1,4,3,0:T(8,128)}, s32[]{:T(128)}) %tuple.55), condition=%wide.while_cond, body=%wide.while_body.sunk | while | flops 2 | bytes 2097785 | solution.py:58
  441.5 5.3 fusion.53
  447.3 17.0 %while.16 = (s32[]{:T(128)}, f32[15,1024,2,16]{1,3,2,0:T(8,128)}, s32[4,4]{1,0:T(4,128)S(1)}, f32[4,8,512,2,16]{2,1,4,3,0:T(8,128)}, s32[]{:T(128)}) while((s32[]{:T(128)}, f32[15,1024,2,16]{1,3,2,0:T(8,128)}, s32[4,4]{1,0:T(4,128)S(1)}, f32[4,8,512,2,16]{2,1,4,3,0:T(8,128)}, s32[]{:T(128)}) %tuple.55), condition=%wide.while_cond, body=%wide.while_body.sunk | while | flops 2 | bytes 2097785 | solution.py:58
  466.0 5.3 fusion.53
  471.7 17.0 %while.16 = (s32[]{:T(128)}, f32[15,1024,2,16]{1,3,2,0:T(8,128)}, s32[4,4]{1,0:T(4,128)S(1)}, f32[4,8,512,2,16]{2,1,4,3,0:T(8,128)}, s32[]{:T(128)}) while((s32[]{:T(128)}, f32[15,1024,2,16]{1,3,2,0:T(8,128)}, s32[4,4]{1,0:T(4,128)S(1)}, f32[4,8,512,2,16]{2,1,4,3,0:T(8,128)}, s32[]{:T(128)}) %tuple.55), condition=%wide.while_cond, body=%wide.while_body.sunk | while | flops 2 | bytes 2097785 | solution.py:58
  490.4 5.3 fusion.53
  496.1 17.0 %while.16 = (s32[]{:T(128)}, f32[15,1024,2,16]{1,3,2,0:T(8,128)}, s32[4,4]{1,0:T(4,128)S(1)}, f32[4,8,512,2,16]{2,1,4,3,0:T(8,128)}, s32[]{:T(128)}) while((s32[]{:T(128)}, f32[15,1024,2,16]{1,3,2,0:T(8,128)}, s32[4,4]{1,0:T(4,128)S(1)}, f32[4,8,512,2,16]{2,1,4,3,0:T(8,128)}, s32[]{:T(128)}) %tuple.55), condition=%wide.while_cond, body=%wide.while_body.sunk | while | flops 2 | bytes 2097785 | solution.py:58
  514.8 5.3 fusion.53
  520.3 24.4 %all_to_all.23 = f32[16,4,2,16,128]{4,3,1,2,0:T(8,128)S(1)} all-to-all(f32[16,4,2,16,128]{4,3,1,2,0:T(8,128)S(1)} %broadcast_multiply_fusion), channel_id=1, replica_groups=mesh['sensor_0'=4,'sensor_1'=2,'chan'=16] {'chan'}, dimensions={0} | all-to-all | bytes 2097152 | tf_op jit(solution)/shard_map/all_to_all | solution.py:34
  (464 shorter events, 313.3 us)
Async XLA Ops:
  13.9 20.7 %all-to-all-start = ((f32[16,1,8192]{2,1,0:T(1,128)}), f32[16,1,8192]{2,1,0:T(1,128)S(1)}, u32[]{:S(2)}, u32[]{:S(2)}) async-start(f32[16,1,8192]{2,1,0:T(1,128)} %reshape.188), calls=%async_computation | async-start | bytes 1048576 | tf_op jit(solution)/shard_map/all_to_all | solution.py:90
  23.2 47.4 %all-gather.3.cloned.1.call-start = ((), (), s32[]{:S(2)}) async-start(), calls=%async_computation.2 | async-start | bytes 1572864 | tf_op jit(solution)/shard_map/all_gather | solution.py:23
  45.9 27.8 %copy-start.1 = (s32[64]{0:T(128)S(1)}, s32[64]{0:T(128)}, u32[]{:S(2)}) copy-start(s32[64]{0:T(128)} %param.7) | copy-start | bytes 772
  45.9 27.9 %copy-start.2 = (s32[64]{0:T(128)S(1)}, s32[64]{0:T(128)}, u32[]{:S(2)}) copy-start(s32[64]{0:T(128)} %param.6) | copy-start | bytes 772
  46.8 33.1 %copy-start = (f32[8,512,2,16]{1,0,3,2:T(8,128)S(1)}, f32[8,512,2,16]{1,0,3,2:T(8,128)}, u32[]{:S(2)}) copy-start(f32[8,512,2,16]{1,0,3,2:T(8,128)} %maximum_bitcast_fusion.3) | copy-start | bytes 1572868
  46.8 74.6 %all-gather.5.cloned.1.call-start = ((), (), s32[]{:S(2)}) async-start(), calls=%async_computation.3 | async-start | bytes 5242880 | tf_op jit(solution)/shard_map/all_gather | solution.py:23
  71.7 8.2 %collective-permute-start = (f32[7,512,2,16]{1,0,3,2:T(8,128)S(1)}, f32[7,512,2,16]{1,0,3,2:T(8,128)S(1)}, u32[]{:S(2)}, u32[]{:S(2)}) collective-permute-start(f32[7,512,2,16]{1,0,3,2:T(8,128)S(1)} %slice.79), channel_id=1, source_target_pairs={{15,0},{0,1},{1,2},{2,3},{3,4},{4,5},{5,6},{6,7},{7,8},{8,9},{9,10... | collective-permute-start | bytes 1376264 | tf_op jit(solution)/shard_map/ppermute | solution.py:18
Sparse Core Ops, SparseCore 0:
  46.9 23.5 all-gather.2
  72.2 49.1 all-gather.4
where the time goes:
time: 557 us; the launch traced here: 552 us
  local copies, waits for them, and re-layouts  325 us (58%)
  matrix products  89.8 us (16%)
  waiting for transfers between devices  69.9 us (13%)
  blocking collectives  24.4 us (4%)
  other arithmetic  16.5 us (3%)
  between operations  13.6 us (2%)
  starting transfers between devices  11.6 us (2%)
    gather x256, local copies, waits for them, and re-layouts  271 us
    dot_general x16, matrix products, one_block(): jnp.einsum('akp,kq->apq', left_rows, flattened, precision=lax.Precision.H...  84.6 us
    all_gather x2, waiting for transfers between devices, whole_of(): x = lax.all_gather(x, axis, axis=dim, tiled=True)  62.4 us
    reshape x16, local copies, waits for them, and re-layouts, one_alpha(): return shifted.reshape(chans * length, 2 * sensors_here)  27.9 us
    all_to_all x1, blocking collectives, sent_and_summed(): tiles = lax.all_to_all(in_blocks(x, dim, count), axis, 0, 0, tiled=True)  24.4 us
    unnamed x9, local copies, waits for them, and re-layouts  12.5 us
  transfers between devices with their start and end apart: 4, of which 4 were waited for; matrix products, arithmetic and copies ran while one was open for 2% of the time, Pallas kernels for 0%

commit v1 on v0

v1 whole, which is shorter than its diff:
```python
import math

import jax
import jax.numpy as jnp
import ml_dtypes
import numpy as np
from jax import lax
from jax.experimental import pallas as pl
from jax.experimental.pallas import tpu as pltpu
from jax.sharding import Mesh
from jax.sharding import PartitionSpec as P

CHANNELS = 128
BLOCKS = 512
ALPHAS = 64
SHIFTS = 8
FLOOR = 0.1
F32 = jnp.float32
BF16 = jnp.bfloat16
VMEM = pl.BlockSpec(memory_space=pltpu.VMEM)
LIMIT = pltpu.CompilerParams(vmem_limit_bytes=48 * 2**20)


def halves(table):
    high = table.astype(ml_dtypes.bfloat16)
    low = (table - high.astype(np.float64)).astype(ml_dtypes.bfloat16)
    return high, low


def channel_table():
    n = np.arange(CHANNELS)
    window = 0.5 - 0.5 * np.cos(2 * np.pi * n / CHANNELS)
    angle = 2 * np.pi * (n[:, None] * n[None, :] % CHANNELS) / CHANNELS
    cosine = window[:, None] * np.cos(angle) / math.sqrt(CHANNELS)
    sine = window[:, None] * np.sin(angle) / math.sqrt(CHANNELS)
    return np.block([[cosine, -sine], [sine, cosine]])


def block_table():
    n = np.arange(BLOCKS)
    angle = 2 * np.pi * (n[:, None] * n[None, :] % BLOCKS) / BLOCKS
    return np.concatenate([np.cos(angle), np.sin(angle)], 0) / math.sqrt(BLOCKS)


def split(x):
    high = x.astype(BF16)
    return high, (x - high.astype(F32)).astype(BF16)


def dot3(a, b, dims):
    def one(u, v):
        return lax.dot_general(u, v, (dims, ((), ())), preferred_element_type=F32)

    return one(a[0], b[0]) + (one(a[0], b[1]) + one(a[1], b[0]))


def lane_block(shape, width):
    return lax.broadcasted_iota(jnp.int32, shape, len(shape) - 1) // width % 2


def swap_blocks(tiles):
    tiles = list(tiles)
    for bit in (1, 2, 4, 8):
        width = 8 * bit
        upper = lane_block(tiles[0].shape, width) == 1
        for i in range(16):
            if i & bit:
                continue
            a, b = tiles[i], tiles[i | bit]
            axis = a.ndim - 1
            tiles[i] = jnp.where(upper, pltpu.roll(b, width, axis), a)
            tiles[i | bit] = jnp.where(upper, b, pltpu.roll(a, 128 - width, axis))
    return tiles


def demod_kernel(x_ref, high_ref, low_ref, out_ref, mid_ref):
    sensors, blocks = x_ref.shape[1], x_ref.shape[2]
    rows = sensors * blocks
    x = jnp.concatenate([x_ref[0].reshape(rows, 128), x_ref[1].reshape(rows, 128)], 1)
    mid_ref[...] = dot3(split(x), (high_ref[...], low_ref[...]), ((1,), (0,)))
    for part in range(2):
        for m in range(0, blocks, 8):
            tiles = [
                mid_ref[s * blocks + m : s * blocks + m + 8, part * 128 : part * 128 + 128]
                for s in range(sensors)
            ]
            for dest, tile in enumerate(swap_blocks(tiles)):
                out_ref[dest, part, m : m + 8, :] = tile


def white_kernel(d_ref, high_ref, low_ref, out_ref):
    parts = [d_ref[:, part].reshape(BLOCKS, 128) for part in range(2)]
    table = (high_ref[...], low_ref[...])
    u = dot3(table, split(jnp.concatenate(parts, 1)), ((1,), (0,)))
    real = u[:BLOCKS, :128] + u[BLOCKS:, 128:]
    imag = u[:BLOCKS, 128:] - u[BLOCKS:, :128]
    scale = 1.0 / jnp.sqrt(real * real + imag * imag + FLOOR)
    u = dot3(table, split(jnp.concatenate([real * scale, imag * scale], 1)), ((1,), (0,)))
    out_ref[:, 0] = (u[:BLOCKS, :128] - u[BLOCKS:, 128:]).reshape(16, 32, 128)
    out_ref[:, 1] = (u[:BLOCKS, 128:] + u[BLOCKS:, :128]).reshape(16, 32, 128)


def turn_kernel(r_ref, out_ref):
    for part in range(2):
        for m in range(0, 32, 8):
            tiles = [r_ref[i, part, m : m + 8, :] for i in range(16)]
            for s, tile in enumerate(swap_blocks(tiles)):
                out_ref[s, part, m : m + 8, :] = tile


def gram_kernel(a_ref, b_ref, ehigh_ref, elow_ref, out_ref, p_ref):
    def one_block(m, carry):
        left = []
        for part in range(2):
            rows = []
            for a in range(32):
                row = a_ref[pl.ds(a * 64 + part * 32 + m, 1), :]
                tile = jnp.broadcast_to(row, (8, 128))
                rows.append(pltpu.roll(tile, 0, 1, stride=1, stride_axis=0))
            left.append(jnp.concatenate(rows, 0))
        left = split(jnp.concatenate(left, 1))
        real = b_ref[pl.ds(m, 64, stride=64), :]
        imag = b_ref[pl.ds(32 + m, 64, stride=64), :]
        upper = jnp.concatenate([real, imag], 1)
        under = jnp.concatenate([-imag, real], 1)
        rows = []
        for x in range(4):
            rows += [upper[x * 16 : x * 16 + 16], under[x * 16 : x * 16 + 16]]
        right = split(jnp.concatenate(rows, 0))
        product = dot3(left, right, ((1,), (1,)))
        p_ref[:, pl.ds(pl.multiple_of(m * 8, 8), 8), :] = product.reshape(32, 8, 128)
        return carry

    lax.fori_loop(0, 32, one_block, 0)
    table = (ehigh_ref[...], elow_ref[...])

    def one_sensor(a, carry):
        t = dot3(table, split(p_ref[a]), ((1,), (0,)))
        cosine, sine = t[:64], t[64:]
        odd = lane_block(sine.shape, 16) == 1
        g = cosine + jnp.where(odd, -pltpu.roll(sine, 16, 1), pltpu.roll(sine, 112, 1))
        for dest in range(16):
            out_ref[dest, a] = g[dest * 4 : dest * 4 + 4]
        return carry

    lax.fori_loop(0, 32, one_sensor, 0)


def call(kernel, out_shape, scratch=()):
    return pl.pallas_call(
        kernel,
        out_shape=jax.ShapeDtypeStruct(out_shape, F32),
        out_specs=VMEM,
        scratch_shapes=list(scratch),
        compiler_params=LIMIT,
    )


def phases(bins, offsets, first):
    m = first + jnp.arange(32, dtype=jnp.int32)
    angle = (bins[:, None] * m[None, :] % BLOCKS).astype(F32) * (2.0 * math.pi / BLOCKS)
    both = jnp.stack([jnp.cos(angle), jnp.sin(angle)]) * (1.0 / 256.0)
    chosen = offsets[:, None] == jnp.arange(SHIFTS, dtype=jnp.int32)[None, :]
    table = jnp.where(chosen[None, :, None, :], both[:, :, :, None], 0.0)
    table = table.reshape(2 * ALPHAS, 32 * SHIFTS)
    high = lax.reduce_precision(table, 8, 7)
    return high.astype(BF16), (table - high).astype(BF16)


def on_device(samples, bins, offsets):
    chan = lax.axis_index("chan")
    wide = lax.axis_index("z")
    e_high, e_low = phases(bins, offsets, chan * 32)
    chunk = (16, 2, 32, 128)
    demod = call(demod_kernel, chunk, [pltpu.VMEM((512, 256), F32)])(
        samples, *halves(channel_table())
    )
    received = lax.all_to_all(demod, "chan", 0, 0, tiled=True)
    white = call(white_kernel, chunk)(received, *halves(block_table()))
    received = lax.all_to_all(white, "chan", 0, 0, tiled=True)
    own = call(turn_kernel, chunk)(received)
    other = lax.ppermute(own, "z", [(0, 1), (1, 0)])
    first = wide == 0
    left = jnp.concatenate([jnp.where(first, own, other), jnp.where(first, other, own)], 0)
    right = lax.all_gather(own, "x", axis=0, tiled=True)
    part = call(gram_kernel, (16, 32, 4, 128), [pltpu.VMEM((32, 256, 128), F32)])(
        left.reshape(-1, 128), right.reshape(-1, 128), e_high, e_low
    )
    part = jnp.sum(lax.all_to_all(part[:, None], "chan", 0, 0, tiled=True), axis=0)
    part = part.reshape(2, 16, 4, 128)
    mine = jnp.where(first, part[0], part[1])
    theirs = lax.ppermute(jnp.where(first, part[1], part[0]), "z", [(0, 1), (1, 0)])
    low = jnp.where(first, mine, theirs).reshape(16, 4, 4, 2, 16)
    high = jnp.where(first, theirs, mine).reshape(16, 4, 4, 2, 16)
    both = jnp.stack([low, high], 4)
    return jnp.transpose(both, (1, 3, 0, 2, 4, 5)).reshape(4, 2, 16, 128)


def solution(mesh):
    finer = Mesh(mesh.devices.reshape(4, 2, mesh.shape["chan"]), ("x", "z", "chan"))
    sensor = ("x", "z")
    return jax.shard_map(
        on_device,
        mesh=finer,
        in_specs=(P(None, sensor, "chan", None), P(), P()),
        out_specs=P("chan", None, sensor, None),
        check_vma=False,
    )
```

time: 557 us -> 140 us (0.25)
  local copies, waits for them, and re-layouts: 325 us -> 7.36 us
  matrix products: 89.8 us -> 0 us
  waiting for transfers between devices: 69.9 us -> 27.9 us
  blocking collectives: 24.4 us -> 59.8 us
  Pallas kernels: 0 us -> 26.5 us
  other arithmetic: 16.5 us -> 1.95 us
  starting transfers between devices: 11.6 us -> 1.27 us
    gather x256 -> x0, local copies, waits for them, and re-layouts: 271 us -> none
    dot_general x18 -> x0, matrix products: 89.8 us -> none  [the longest x16 84.6 us: one_block(): jnp.einsum('akp,kq->apq', left_rows, flattened, precision=lax.Precision.H...]
    all_gather x2 -> x1, waiting for transfers between devices: 62.4 us -> 14 us  [on_device(): right = lax.all_gather(own, 'x', axis=0, tiled=True)]
    all_to_all x1 -> x3, blocking collectives: 24.4 us -> 59.8 us  [the longest x1 24.4 us: on_device(): lax.all_to_all(part[:, None], 'chan', 0, 0, tiled=True)]
    reshape x20 -> x1, local copies, waits for them, and re-layouts: 30.3 us -> 1.28 us  [on_device(): return jnp.transpose(both, (1, 3, 0, 2, 4, 5)).reshape(4, 2, 16, 128)]
    pallas_call x0 -> x4, Pallas kernels: none -> 26.5 us  [the longest x1 19.8 us: on_device(): call(gram_kernel, (16, 32, 4, 128), [pltpu.VMEM((32, 256, 128), F32)])]
    all_to_all x1 -> x0, starting transfers between devices: 9.3 us -> none  [on_device(): lax.all_to_all(demodulates, 'chan', split_axis=2, concat_axis=3, tiled=True)]
    unnamed x9 -> x16, local copies, waits for them, and re-layouts: 12.5 us -> 4.61 us
  transfers between devices with their start and end apart: 4 -> 3, of which waited for: 4 -> 3; matrix products, arithmetic and copies ran while one was open for 2% -> 1% of each run, Pallas kernels for 0% -> 0%
where the time goes in v1:
time: 140 us; the launch traced here: 138 us
  blocking collectives  59.8 us (43%)
  waiting for transfers between devices  27.9 us (20%)
  Pallas kernels  26.5 us (19%)
  between operations  13.6 us (10%)
  local copies, waits for them, and re-layouts  7.36 us (5%)
  other arithmetic  1.95 us (1%)
    all_to_all x1, blocking collectives, on_device(): lax.all_to_all(part[:, None], 'chan', 0, 0, tiled=True)  24.4 us
    all_to_all x1, blocking collectives, on_device(): received = lax.all_to_all(demod, 'chan', 0, 0, tiled=True)  20.5 us
    pallas_call x1, Pallas kernels, on_device(): call(gram_kernel, (16, 32, 4, 128), [pltpu.VMEM((32, 256, 128), F32)])  19.8 us
    all_to_all x1, blocking collectives, on_device(): received = lax.all_to_all(white, 'chan', 0, 0, tiled=True)  15 us
    all_gather x1, waiting for transfers between devices, on_device(): right = lax.all_gather(own, 'x', axis=0, tiled=True)  14 us
    ppermute x1, waiting for transfers between devices, on_device(): other = lax.ppermute(own, 'z', [(0, 1), (1, 0)])  11.5 us
    unnamed x16, local copies, waits for them, and re-layouts  4.61 us
    pallas_call x1, Pallas kernels, on_device(): white = call(white_kernel, chunk)(received, *halves(block_table()))  3.5 us
  transfers between devices with their start and end apart: 3, of which 3 were waited for; matrix products, arithmetic and copies ran while one was open for 1% of the time, Pallas kernels for 0%

profile of v1, /device:TPU:1, one launch (start us, length us, event | category | flops | bytes accessed | tf_op | source)
XLA Modules:
  0.0 138.4 jit_solution(3234665278245674454)
XLA Ops:
  6.5 0.0 copy-start.1
  6.5 0.0 copy-start.2
  6.5 0.0 all-gather.2.cloned.1.call-start
  6.5 0.0 copy-start.3
  6.5 1.2 copy-done.3
  7.7 0.0 copy-start.4
  7.7 0.9 copy-done.4
  8.6 0.0 copy-start.5
  8.6 0.9 copy-done.5
  9.5 1.0 shard_map.73
  10.5 20.5 %all_to_all.15.d_ref = f32[16,2,32,128]{3,2,1,0:T(8,128)S(1)} all-to-all(f32[16,2,32,128]{3,2,1,0:T(8,128)S(1)} %shard_map.73), channel_id=1, replica_groups=mesh['x'=4,'z'=2,'chan'=16] {'chan'}, dimensions={0} | all-to-all | bytes 1048576 | tf_op jit(solution)/shard_map/all_to_all | solution.py:178
  31.0 0.0 copy-done.1
  31.0 0.0 copy-done.2
  31.0 3.5 %shard_map.74 = f32[16,2,32,128]{3,2,1,0:T(8,128)S(1)} custom-call(f32[16,2,32,128]{3,2,1,0:T(8,128)S(1)} %all_to_all.15.d_ref, bf16[1024,512]{1,0:T(8,128)(2,1)S(1)} %copy-done.2, bf16[1024,512]{1,0:T(8,128)(2,1)S(1)} %copy-done.1), custom_call_target="tpu_custom_call" | custom-call | tf_op jit(solution)/shard_map/pallas_call | solution.py:179
  34.5 0.0 copy-start.7
  34.5 0.0 copy-start.6
  34.6 15.0 %all_to_all.16.r_ref = f32[16,2,32,128]{3,2,1,0:T(8,128)S(1)} all-to-all(f32[16,2,32,128]{3,2,1,0:T(8,128)S(1)} %shard_map.74), channel_id=1, replica_groups=mesh['x'=4,'z'=2,'chan'=16] {'chan'}, dimensions={0} | all-to-all | bytes 1048576 | tf_op jit(solution)/shard_map/all_to_all | solution.py:180
  49.6 2.2 %shard_map.75 = f32[16,2,32,128]{3,2,1,0:T(8,128)} custom-call(f32[16,2,32,128]{3,2,1,0:T(8,128)S(1)} %all_to_all.16.r_ref), custom_call_target="tpu_custom_call" | custom-call | tf_op jit(solution)/shard_map/pallas_call | solution.py:181
  51.7 0.0 all-gather.2.cloned.1.call-update
  51.8 0.0 copy-done.7
  51.8 0.0 copy-done.6
  51.8 0.2 fusion.5
  51.9 0.8 collective-permute-start
  52.8 0.1 broadcast_select_fusion
  52.9 0.2 select_n.77
  53.1 0.1 copy.21
  53.2 11.5 %collective-permute-done = f32[16,2,32,128]{3,2,1,0:T(8,128)S(1)} collective-permute-done((f32[16,2,32,128]{3,2,1,0:T(8,128)}, f32[16,2,32,128]{3,2,1,0:T(8,128)S(1)}, u32[]{:S(2)}, u32[]{:S(2)}) %collective-permute-start) | collective-permute-done | bytes 524320 | tf_op jit(solution)/shard_map/ppermute | solution.py:182
  64.7 1.2 broadcast_select_fusion.2
  65.9 0.1 pad_maximum_fusion
  66.0 14.0 %all-gather.2.cloned.1.call-done = f32[64,2,32,128]{3,2,1,0:T(8,128)} async-done(((f32[16,2,32,128]{3,2,1,0:T(8,128)}), f32[64,2,32,128]{3,2,1,0:T(8,128)}) %all-gather.2.cloned.1.call-update) | async-done | bytes 2097168 | tf_op jit(solution)/shard_map/all_gather | solution.py:185
  80.0 0.0 copy-start
  80.0 1.6 %copy-done = f32[64,2,32,128]{3,2,1,0:T(8,128)S(1)} copy-done((f32[64,2,32,128]{3,2,1,0:T(8,128)S(1)}, f32[64,2,32,128]{3,2,1,0:T(8,128)}, u32[]{:S(2)}) %copy-start) | copy-done | bytes 2097176
  81.5 19.8 %shard_map.76 = f32[16,32,4,128]{3,2,1,0:T(4,128)S(1)} custom-call(f32[2048,128]{1,0:T(8,128)S(1)} %bitcast.21, f32[4096,128]{1,0:T(8,128)S(1)} %bitcast.23, bf16[128,256]{1,0:T(8,128)(2,1)S(1)} %get-tuple-element.8.ehigh_ref, bf16[128,256]{1,0:T(8,128)(2,1)S(1)} %get-tuple-element.7.elow_ref), custom_call_target="tpu_custom_call" | custom-call | tf_op jit(solution)/shard_map/pallas_call | solution.py:186
  101.4 24.4 %all_to_all.17 = f32[16,1,32,4,128]{4,3,2,1,0:T(4,128)S(1)} all-to-all(f32[16,1,32,4,128]{4,3,2,1,0:T(4,128)S(1)} %bitcast.22), channel_id=1, replica_groups=mesh['x'=4,'z'=2,'chan'=16] {'chan'}, dimensions={0} | all-to-all | bytes 2097152 | tf_op jit(solution)/shard_map/all_to_all | solution.py:189
  125.8 0.1 bitcast_reduce_fusion
  125.9 0.5 collective-permute-start.1
  126.3 2.4 %collective-permute-done.1 = f32[16,4,128]{2,1,0:T(4,128)S(1)} collective-permute-done((f32[16,4,128]{2,1,0:T(4,128)S(1)}, f32[16,4,128]{2,1,0:T(4,128)S(1)}, u32[]{:S(2)}, u32[]{:S(2)}) %collective-permute-start.1) | collective-permute-done | bytes 32800 | tf_op jit(solution)/shard_map/ppermute | solution.py:192
  128.8 0.4 stack_reshape.7
  129.2 0.4 stack_reshape.6
  129.5 0.3 maximum_bitcast_fusion
  129.8 0.4 copy.27
  130.2 1.3 reshape.197
  (9 shorter events, 0.1 us)
Async XLA Ops:
  6.5 24.5 %copy-start.1 = (bf16[1024,512]{1,0:T(8,128)(2,1)S(1)}, bf16[1024,512]{1,0:T(8,128)(2,1)}, u32[]{:S(2)}) copy-start(bf16[1024,512]{1,0:T(8,128)(2,1)} %constant.44.clone.low_ref) | copy-start | bytes 3145732
  6.5 24.5 %copy-start.2 = (bf16[1024,512]{1,0:T(8,128)(2,1)S(1)}, bf16[1024,512]{1,0:T(8,128)(2,1)}, u32[]{:S(2)}) copy-start(bf16[1024,512]{1,0:T(8,128)(2,1)} %constant.43.clone.high_ref) | copy-start | bytes 3145732
  6.5 73.4 %all-gather.2.cloned.1.call-start = ((), (), s32[]{:S(2)}) async-start(), calls=%async_computation.3 | async-start | bytes 2621440 | tf_op jit(solution)/shard_map/all_gather | solution.py:185
  6.5 1.2 copy-start.3
  7.7 0.9 copy-start.4
  8.6 0.9 copy-start.5
  34.5 17.2 %copy-start.7 = (s32[64]{0:T(128)S(1)}, s32[64]{0:T(128)}, u32[]{:S(2)}) copy-start(s32[64]{0:T(128)} %param.9) | copy-start | bytes 772
  34.5 17.2 %copy-start.6 = (s32[64]{0:T(128)S(1)}, s32[64]{0:T(128)}, u32[]{:S(2)}) copy-start(s32[64]{0:T(128)} %param.8) | copy-start | bytes 772
  51.9 12.8 %collective-permute-start = (f32[16,2,32,128]{3,2,1,0:T(8,128)}, f32[16,2,32,128]{3,2,1,0:T(8,128)S(1)}, u32[]{:S(2)}, u32[]{:S(2)}) collective-permute-start(f32[16,2,32,128]{3,2,1,0:T(8,128)} %shard_map.75), channel_id=1, source_target_pairs={{0,16},{16,0},{1,17},{17,1},{2,18},{18,2},{3,19},{19,3},{4,20},{20... | collective-permute-start | bytes 1572872 | tf_op jit(solution)/shard_map/ppermute | solution.py:182
  80.0 1.6 %copy-start = (f32[64,2,32,128]{3,2,1,0:T(8,128)S(1)}, f32[64,2,32,128]{3,2,1,0:T(8,128)}, u32[]{:S(2)}) copy-start(f32[64,2,32,128]{3,2,1,0:T(8,128)} %all-gather.2.cloned.1.call-done) | copy-start | bytes 6291460
  125.9 2.8 %collective-permute-start.1 = (f32[16,4,128]{2,1,0:T(4,128)S(1)}, f32[16,4,128]{2,1,0:T(4,128)S(1)}, u32[]{:S(2)}, u32[]{:S(2)}) collective-permute-start(f32[16,4,128]{2,1,0:T(4,128)S(1)} %select_bitcast_fusion), channel_id=1, source_target_pairs={{0,16},{16,0},{1,17},{17,1},{2,18},{18,2},{3,19},{19,3},{4,20},{20... | collective-permute-start | bytes 98312 | tf_op jit(solution)/shard_map/ppermute | solution.py:192
Sparse Core Ops, SparseCore 0:
  51.9 28.0 all-gather.1

commit v2 on v1

v2 whole, which is shorter than its diff:
```python
import math

import jax
import jax.numpy as jnp
import ml_dtypes
import numpy as np
from jax import lax
from jax.experimental import pallas as pl
from jax.experimental.pallas import tpu as pltpu
from jax.sharding import Mesh
from jax.sharding import PartitionSpec as P

CHANNELS = 128
BLOCKS = 512
ALPHAS = 64
SHIFTS = 8
FLOOR = 0.1
F32 = jnp.float32
BF16 = jnp.bfloat16
VMEM = pl.BlockSpec(memory_space=pltpu.VMEM)


def halves(table):
    high = table.astype(ml_dtypes.bfloat16)
    low = (table - high.astype(np.float64)).astype(ml_dtypes.bfloat16)
    return high, low


def channel_table():
    n = np.arange(CHANNELS)
    window = 0.5 - 0.5 * np.cos(2 * np.pi * n / CHANNELS)
    angle = 2 * np.pi * (n[:, None] * n[None, :] % CHANNELS) / CHANNELS
    cosine = window[:, None] * np.cos(angle) / math.sqrt(CHANNELS)
    sine = window[:, None] * np.sin(angle) / math.sqrt(CHANNELS)
    return np.block([[cosine, -sine], [sine, cosine]])


def block_table():
    n = np.arange(BLOCKS).reshape(16, 4, 8).transpose(1, 0, 2).reshape(-1)
    angle = 2 * np.pi * (n[:, None] * n[None, :] % BLOCKS) / BLOCKS
    return np.concatenate([np.cos(angle), np.sin(angle)], 0) / math.sqrt(BLOCKS)


def split(x):
    high = x.astype(BF16)
    return high, (x - high.astype(F32)).astype(BF16)


def dot3(a, b, dims):
    def one(u, v):
        return lax.dot_general(u, v, (dims, ((), ())), preferred_element_type=F32)

    return one(a[0], b[0]) + (one(a[0], b[1]) + one(a[1], b[0]))


def lane_block(shape, width):
    return lax.broadcasted_iota(jnp.int32, shape, len(shape) - 1) // width % 2


def swap_blocks(tiles):
    tiles = list(tiles)
    for bit in (1, 2, 4, 8):
        width = 8 * bit
        upper = lane_block(tiles[0].shape, width) == 1
        for i in range(16):
            if i & bit:
                continue
            a, b = tiles[i], tiles[i | bit]
            axis = a.ndim - 1
            tiles[i] = jnp.where(upper, pltpu.roll(b, width, axis), a)
            tiles[i | bit] = jnp.where(upper, b, pltpu.roll(a, 128 - width, axis))
    return tiles


def fill(copies, start=True):
    for copy in copies:
        copy.start() if start else copy.wait()


def remote(src, dst, send, recv, **where):
    return pltpu.make_async_remote_copy(
        src_ref=src,
        dst_ref=dst,
        send_sem=send,
        recv_sem=recv,
        device_id=where,
        device_id_type=pl.DeviceIdType.MESH,
    )


def greet(peers):
    barrier = pltpu.get_barrier_semaphore()
    for where in peers:
        pl.semaphore_signal(barrier, device_id=where, device_id_type=pl.DeviceIdType.MESH)
    return lambda: pl.semaphore_wait(barrier, len(peers))


def front_kernel(
    x_ref, chigh_ref, clow_ref, thigh_hbm, tlow_hbm, right_ref, other_ref,
    mid_ref, made_ref, got_ref, back_ref, land_ref, thigh_ref, tlow_ref,
    table_sem, send1, recv1, send2, recv2, sendx, recvx, sendf, recvf, sendz, recvz,
):
    chan, x, z = lax.axis_index("chan"), lax.axis_index("x"), lax.axis_index("z")
    after, before = lax.rem(x + 1, 4), lax.rem(x + 3, 4)
    peers = [lax.rem(chan + o, 16) for o in range(1, 16)]
    arrived = greet(
        [{"chan": c} for c in peers] + [{"x": after}, {"x": before}, {"z": 1 - z}]
    )
    tables = [
        pltpu.make_async_copy(thigh_hbm, thigh_ref, table_sem.at[0]),
        pltpu.make_async_copy(tlow_hbm, tlow_ref, table_sem.at[1]),
    ]
    fill(tables)
    part = jnp.concatenate([x_ref[0].reshape(512, 128), x_ref[1].reshape(512, 128)], 1)
    mid_ref[...] = dot3(split(part), (chigh_ref[...], clow_ref[...]), ((1,), (0,)))
    for c in range(2):
        for mc in range(4):
            tiles = [
                mid_ref[s * 32 + mc * 8 : s * 32 + mc * 8 + 8, c * 128 : c * 128 + 128]
                for s in range(16)
            ]
            for dest, tile in enumerate(swap_blocks(tiles)):
                made_ref[dest, mc, c] = tile
    arrived()

    def first_out(o):
        peer = lax.rem(chan + o, 16)
        return remote(made_ref.at[peer], got_ref.at[chan], send1.at[o], recv1.at[chan], chan=peer)

    def first_in(o):
        peer = lax.rem(chan + o, 16)
        return remote(made_ref.at[peer], got_ref.at[peer], send1.at[o], recv1.at[peer], chan=peer)

    @pl.loop(1, 16)
    def _(o):
        first_out(o).start()

    got_ref[chan] = made_ref[chan]
    fill(tables, False)

    @pl.loop(1, 16)
    def _(o):
        first_in(o).wait_recv()

    def gathered(c):
        return jnp.concatenate([got_ref[:, mc, c].reshape(128, 128) for mc in range(4)], 0)

    u = dot3(
        (thigh_ref[...], tlow_ref[...]),
        split(jnp.concatenate([gathered(0), gathered(1)], 1)),
        ((1,), (0,)),
    )
    real = u[:BLOCKS, :128] + u[BLOCKS:, 128:]
    imag = u[:BLOCKS, 128:] - u[BLOCKS:, :128]
    scale = 1.0 / jnp.sqrt(real * real + imag * imag + FLOOR)
    white = split(jnp.concatenate([real * scale, imag * scale], 1))

    def second_out(o, mc):
        peer = lax.rem(chan + o, 16)
        return remote(
            back_ref.at[peer, mc], land_ref.at[chan, mc], send2.at[mc, o], recv2.at[mc, chan], chan=peer
        )

    def second_in(o, mc):
        peer = lax.rem(chan + o, 16)
        return remote(
            back_ref.at[peer, mc], land_ref.at[peer, mc], send2.at[mc, o], recv2.at[mc, peer], chan=peer
        )

    for mc in range(4):
        ups = []
        for row in (mc * 128, BLOCKS + mc * 128):
            table = (thigh_ref[row : row + 128, :], tlow_ref[row : row + 128, :])
            ups.append(dot3(table, white, ((1,), (0,))))
        cosine, sine = ups
        back_ref[:, mc, 0] = (cosine[:, :128] - sine[:, 128:]).reshape(16, 8, 128)
        back_ref[:, mc, 1] = (cosine[:, 128:] + sine[:, :128]).reshape(16, 8, 128)

        @pl.loop(1, 16)
        def _(o, mc=mc):
            second_out(o, mc).start()

        land_ref[chan, mc] = back_ref[chan, mc]

    def to_x(mc, way):
        peer = after if way == 0 else before
        return remote(
            right_ref.at[x, mc], right_ref.at[x, mc], sendx.at[way, mc], recvx.at[way, mc], x=peer
        )

    def from_x(mc, way):
        peer = before if way == 0 else after
        return remote(
            right_ref.at[peer, mc], right_ref.at[peer, mc], sendx.at[way, mc], recvx.at[way, mc], x=peer
        )

    def passed(mc):
        source, peer = (before, after) if mc % 2 == 0 else (after, before)
        return remote(
            right_ref.at[source, mc], right_ref.at[source, mc], sendf.at[mc], recvf.at[mc], x=peer
        )

    def passed_in(mc):
        far = lax.rem(x + 2, 4)
        return remote(right_ref.at[far, mc], right_ref.at[far, mc], sendf.at[mc], recvf.at[mc], x=after)

    def to_z(mc):
        return remote(right_ref.at[x, mc], other_ref.at[mc], sendz.at[mc], recvz.at[mc], z=1 - z)

    for mc in range(4):

        @pl.loop(1, 16)
        def _(o, mc=mc):
            second_in(o, mc).wait_recv()

        for c in range(2):
            tiles = [land_ref[i, mc, c] for i in range(16)]
            for s, tile in enumerate(swap_blocks(tiles)):
                right_ref[x, mc, s, c] = tile
        to_x(mc, 0).start()
        to_x(mc, 1).start()
        to_z(mc).start()
    for mc in range(4):
        from_x(mc, mc % 2).wait_recv()
        passed(mc).start()
    for mc in range(4):
        from_x(mc, 1 - mc % 2).wait_recv()
        to_z(mc).wait_recv()
        passed_in(mc).wait_recv()

    @pl.loop(1, 16)
    def _(o):
        first_out(o).wait_send()
        for mc in range(4):
            second_out(o, mc).wait_send()

    for mc in range(4):
        to_x(mc, 0).wait_send()
        to_x(mc, 1).wait_send()
        to_z(mc).wait_send()
        passed(mc).wait_send()


def gram_kernel(right_ref, other_ref, ehigh_ref, elow_ref, out_ref, p_ref):
    own = lax.axis_index("x") * 1024

    def one_block(m, carry):
        at = m // 8 * 256 + m % 8
        left = []
        for part in range(2):
            rows = []
            for a in range(32):
                start = at + a % 16 * 16 + part * 8
                ref, start = (right_ref, start + own) if a < 16 else (other_ref, start)
                tile = jnp.broadcast_to(ref[pl.ds(start, 1), :], (8, 128))
                rows.append(pltpu.roll(tile, 0, 1, stride=1, stride_axis=0))
            left.append(jnp.concatenate(rows, 0))
        left = split(jnp.concatenate(left, 1))
        rows = []
        for x in range(4):
            real = right_ref[pl.ds(at + x * 1024, 16, stride=16), :]
            imag = right_ref[pl.ds(at + x * 1024 + 8, 16, stride=16), :]
            rows.append(jnp.concatenate([real, imag], 1))
            rows.append(jnp.concatenate([-imag, real], 1))
        right = split(jnp.concatenate(rows, 0))
        product = dot3(left, right, ((1,), (1,)))
        p_ref[:, pl.ds(pl.multiple_of(m * 8, 8), 8), :] = product.reshape(32, 8, 128)
        return carry

    lax.fori_loop(0, 32, one_block, 0, unroll=2)
    table = (ehigh_ref[...], elow_ref[...])
    low = lax.broadcasted_iota(jnp.int32, (8, 128), 0) < 4

    def one_pair(pair, carry):
        both = jnp.concatenate([p_ref[pair * 2], p_ref[pair * 2 + 1]], 1)
        t = dot3(table, split(both), ((1,), (0,)))
        gs = []
        for i in range(2):
            cosine, sine = t[:64, i * 128 : i * 128 + 128], t[64:, i * 128 : i * 128 + 128]
            odd = lane_block(sine.shape, 16) == 1
            gs.append(cosine + jnp.where(odd, -pltpu.roll(sine, 16, 1), pltpu.roll(sine, 112, 1)))
        row = pl.ds(pl.multiple_of(lax.rem(pair, 8) * 8, 8), 8)
        for t8 in range(8):
            a0, a1 = (g[t8 * 8 : t8 * 8 + 8] for g in gs)
            out_ref[0, pair // 8, t8, row, :] = jnp.where(low, a0, pltpu.roll(a1, 4, 0))
            out_ref[1, pair // 8, t8, row, :] = jnp.where(low, pltpu.roll(a0, 4, 0), a1)
        return carry

    lax.fori_loop(0, 16, one_pair, 0)


def back_kernel(g_ref, out_ref, pair_ref, sum_ref, all_ref, res_ref, sendp, recvp, sends, recvs):
    chan, z = lax.axis_index("chan"), lax.axis_index("z")
    core, place = lax.rem(chan, 2), chan // 2
    mate = chan + 1 - 2 * core
    peers = [{"chan": mate}]
    for o in range(1, 16):
        peers.append({"z": lax.rem(z + o // 8, 2), "chan": lax.rem(place + o, 8) * 2 + core})
    greet(peers)()

    def to_mate(h):
        return remote(g_ref.at[1 - core, h], pair_ref.at[h], sendp.at[h], recvp.at[h], chan=mate)

    def spread(o):
        to_z, to = lax.rem(z + o // 8, 2), lax.rem(place + lax.rem(o, 8), 8)
        return to_z, to

    def out(o):
        to_z, to = spread(o)
        return remote(
            sum_ref.at[o // 8, to], all_ref.at[z, place], sends.at[o], recvs.at[z, place],
            z=to_z, chan=to * 2 + core,
        )

    def into(o):
        from_z, at = spread(o)
        return remote(
            sum_ref.at[o // 8, at], all_ref.at[from_z, at], sends.at[o], recvs.at[from_z, at],
            z=from_z, chan=at * 2 + core,
        )

    to_mate(1).start()
    to_mate(0).start()
    to_mate(1).wait_recv()
    sum_ref[1] = g_ref[core, 1] + pair_ref[1]

    @pl.loop(8, 16)
    def _(o):
        out(o).start()

    to_mate(0).wait_recv()
    sum_ref[0] = g_ref[core, 0] + pair_ref[0]

    @pl.loop(1, 8)
    def _(o):
        out(o).start()

    all_ref[z, place] = sum_ref[0, place]

    @pl.loop(1, 16)
    def _(o):
        into(o).wait_recv()

    lo, hi = (jnp.sum(all_ref[h], axis=0) for h in range(2))
    odd = lane_block(lo.shape, 16) == 1
    res_ref[0] = jnp.where(odd, pltpu.roll(hi, 16, 1), lo)
    res_ref[1] = jnp.where(odd, hi, pltpu.roll(lo, 112, 1))
    for j in range(4):
        for c in range(2):
            out_ref[j, c] = res_ref[c, pl.ds(j, 16, stride=4), :]

    @pl.loop(1, 16)
    def _(o):
        out(o).wait_send()

    to_mate(0).wait_send()
    to_mate(1).wait_send()


ANY = pl.BlockSpec(memory_space=pl.ANY)
DMA = pltpu.SemaphoreType.DMA


def phases(bins, offsets, first):
    m = first + jnp.arange(32, dtype=jnp.int32)
    angle = (bins[:, None] * m[None, :] % BLOCKS).astype(F32) * (2.0 * math.pi / BLOCKS)
    both = jnp.stack([jnp.cos(angle), jnp.sin(angle)]) * (1.0 / 256.0)
    chosen = offsets[:, None] == jnp.arange(SHIFTS, dtype=jnp.int32)[None, :]
    table = jnp.where(chosen[None, :, None, :], both[:, :, :, None], 0.0)
    table = table.reshape(2 * ALPHAS, 32 * SHIFTS)
    high = lax.reduce_precision(table, 8, 7)
    return high.astype(BF16), (table - high).astype(BF16)


def params(collective=None):
    return pltpu.CompilerParams(
        vmem_limit_bytes=48 * 2**20,
        collective_id=collective,
        has_side_effects=collective is not None,
    )


def on_device(samples, bins, offsets):
    e_high, e_low = phases(bins, offsets, lax.axis_index("chan") * 32)
    chunk = (16, 4, 2, 8, 128)
    right, other = pl.pallas_call(
        front_kernel,
        out_shape=[
            jax.ShapeDtypeStruct((4, 4, 16, 2, 8, 128), F32),
            jax.ShapeDtypeStruct((4, 16, 2, 8, 128), F32),
        ],
        in_specs=[VMEM, VMEM, VMEM, ANY, ANY],
        out_specs=[VMEM, VMEM],
        scratch_shapes=[pltpu.VMEM((512, 256), F32)]
        + [pltpu.VMEM(chunk, F32)] * 4
        + [pltpu.VMEM((2 * BLOCKS, BLOCKS), BF16)] * 2
        + [DMA((2,)), DMA((16,)), DMA((16,)), DMA((4, 16)), DMA((4, 16))]
        + [DMA((2, 4)), DMA((2, 4)), DMA((4,)), DMA((4,)), DMA((4,)), DMA((4,))],
        compiler_params=params(0),
        name="front",
    )(samples, *halves(channel_table()), *halves(block_table()))
    part = pl.pallas_call(
        gram_kernel,
        out_shape=jax.ShapeDtypeStruct((2, 2, 8, 64, 128), F32),
        in_specs=[VMEM] * 4,
        out_specs=VMEM,
        scratch_shapes=[pltpu.VMEM((32, 256, 128), F32)],
        compiler_params=params(),
        name="gram",
    )(right.reshape(-1, 128), other.reshape(-1, 128), e_high, e_low)
    return pl.pallas_call(
        back_kernel,
        out_shape=jax.ShapeDtypeStruct((4, 2, 16, 128), F32),
        in_specs=[VMEM],
        out_specs=VMEM,
        scratch_shapes=[
            pltpu.VMEM((2, 8, 64, 128), F32),
            pltpu.VMEM((2, 8, 64, 128), F32),
            pltpu.VMEM((2, 8, 64, 128), F32),
            pltpu.VMEM((2, 64, 128), F32),
            DMA((2,)), DMA((2,)), DMA((16,)), DMA((2, 8)),
        ],
        compiler_params=params(1),
        name="back",
    )(part)


def solution(mesh):
    finer = Mesh(mesh.devices.reshape(4, 2, mesh.shape["chan"]), ("x", "z", "chan"))
    sensor = ("x", "z")
    return jax.shard_map(
        on_device,
        mesh=finer,
        in_specs=(P(None, sensor, "chan", None), P(), P()),
        out_specs=P("chan", None, sensor, None),
        check_vma=False,
    )
```

time: 140 us -> 79.7 us (0.57)
  blocking collectives: 59.8 us -> 0 us
  Pallas kernels: 26.5 us -> 72.7 us
  waiting for transfers between devices: 27.9 us -> 0 us
  between operations: 13.6 us -> 0.09 us
  local copies, waits for them, and re-layouts: 7.36 us -> 5.01 us
    all_to_all x3 -> x0, blocking collectives: 59.8 us -> none  [the longest x1 24.4 us: on_device(): lax.all_to_all(part[:, None], 'chan', 0, 0, tiled=True)]
    pallas_call x4 -> x3, Pallas kernels: 26.5 us -> 72.7 us  [the longest x1 46.6 us: on_device(): pl.pallas_call(front_kernel, out_shape=[jax.ShapeDtypeStruct((4, 4, 16, 2...]
    all_gather x1 -> x0, waiting for transfers between devices: 14 us -> none  [on_device(): right = lax.all_gather(own, 'x', axis=0, tiled=True)]
    ppermute x2 -> x0, waiting for transfers between devices: 13.9 us -> none  [the longest x1 11.5 us: on_device(): other = lax.ppermute(own, 'z', [(0, 1), (1, 0)])]
    unnamed x16 -> x11, local copies, waits for them, and re-layouts: 4.61 us -> 4.7 us
  transfers between devices with their start and end apart: 3 -> 0, of which waited for: 3 -> 0; matrix products, arithmetic and copies ran while one was open for 1% -> 0% of each run, Pallas kernels for 0% -> 0%
where the time goes in v2:
time: 79.7 us; the launch traced here: 79.4 us
  Pallas kernels  72.7 us (91%)
  local copies, waits for them, and re-layouts  5.01 us (6%)
  other arithmetic  1.66 us (2%)
    pallas_call x1, Pallas kernels, on_device(): pl.pallas_call(front_kernel, out_shape=[jax.ShapeDtypeStruct((4, 4, 16, 2...  46.6 us
    pallas_call x1, Pallas kernels, on_device(): pl.pallas_call(back_kernel, out_shape=jax.ShapeDtypeStruct((4, 2, 16, 128...  13.7 us
    pallas_call x1, Pallas kernels, on_device(): pl.pallas_call(gram_kernel, out_shape=jax.ShapeDtypeStruct((2, 2, 8, 64,...  12.5 us
    unnamed x11, local copies, waits for them, and re-layouts  4.7 us

profile of v2, /device:TPU:1, one launch (start us, length us, event | category | flops | bytes accessed | tf_op | source)
XLA Modules:
  0.0 79.4 jit_solution(4864405861521134560)
XLA Ops:
  0.0 0.0 copy-start
  0.0 0.7 iota_compare_fusion
  0.8 0.8 %fusion.5 = (f32[1,64,32]{1,2,0:T(8,128)S(1)}, f32[1,64,32]{1,2,0:T(8,128)S(1)}) fusion(s32[32]{0:T(128)S(1)} %iota_add_fusion, s32[64]{0:T(128)} %param.8), kind=kLoop, calls=%fused_computation.14 | loop fusion | flops 28672 | bytes 16768 | tf_op jit(solution)/shard_map/cos | solution.py:367
  1.6 0.1 broadcast_select_fusion
  1.7 0.2 select_n.32
  1.9 0.1 copy.11
  2.0 0.0 copy-done
  2.0 0.0 copy-start.1
  2.0 1.2 %copy-done.1 = bf16[1024,512]{1,0:T(8,128)(2,1)S(1)} copy-done((bf16[1024,512]{1,0:T(8,128)(2,1)S(1)}, bf16[1024,512]{1,0:T(8,128)(2,1)}, u32[]{:S(2)}) %copy-start.1) | copy-done | bytes 1048600
  3.3 0.0 copy-start.2
  3.3 1.0 %copy-done.2 = f32[2,16,32,128]{3,2,1,0:T(8,128)S(1)} copy-done((f32[2,16,32,128]{3,2,1,0:T(8,128)S(1)}, f32[2,16,32,128]{3,2,1,0:T(8,128)}, u32[]{:S(2)}) %copy-start.2) | copy-done | bytes 524312
  4.3 0.0 copy-start.3
  4.3 0.9 %copy-done.3 = bf16[256,256]{1,0:T(8,128)(2,1)S(1)} copy-done((bf16[256,256]{1,0:T(8,128)(2,1)S(1)}, bf16[256,256]{1,0:T(8,128)(2,1)}, u32[]{:S(2)}) %copy-start.3) | copy-done | bytes 131096
  5.2 0.0 copy-start.4
  5.2 0.9 %copy-done.4 = bf16[256,256]{1,0:T(8,128)(2,1)S(1)} copy-done((bf16[256,256]{1,0:T(8,128)(2,1)S(1)}, bf16[256,256]{1,0:T(8,128)(2,1)}, u32[]{:S(2)}) %copy-start.4) | copy-done | bytes 131096
  6.1 46.6 %front.1 = (f32[4,4,16,2,8,128]{5,4,3,2,1,0:T(8,128)S(1)}, f32[4,16,2,8,128]{4,3,2,1,0:T(8,128)S(1)}) custom-call(f32[2,16,32,128]{3,2,1,0:T(8,128)S(1)} %copy-done.2, bf16[256,256]{1,0:T(8,128)(2,1)S(1)} %copy-done.4, bf16[256,256]{1,0:T(8,128)(2,1)S(1)} %copy-done.3, bf16[1024,512]{1,0:T(8,128)(2,1)S(1)} %copy-done.1, bf16[1024,512]{1,0:T(8,128)(2,1)S(1)} %copy-done), custom_call_target="tpu_custom_call" | custom-call | tf_op jit(solution)/shard_map/front/pallas_call | solution.py:386
  52.7 12.5 %gram.1.g_ref = f32[2,2,8,64,128]{4,3,2,1,0:T(8,128)S(1)} custom-call(f32[4096,128]{1,0:T(8,128)S(1)} %bitcast.4, f32[1024,128]{1,0:T(8,128)S(1)} %bitcast.5, bf16[128,256]{1,0:T(8,128)(2,1)S(1)} %get-tuple-element.10.ehigh_ref, bf16[128,256]{1,0:T(8,128)(2,1)S(1)} %get-tuple-element.9.elow_ref), custom_call_target="tpu_custom_call" | custom-call | tf_op jit(solution)/shard_map/gram/pallas_call | solution.py:402
  65.2 13.7 %back.1 = f32[4,2,16,128]{3,2,1,0:T(8,128)S(1)} custom-call(f32[2,2,8,64,128]{4,3,2,1,0:T(8,128)S(1)} %gram.1.g_ref), custom_call_target="tpu_custom_call" | custom-call | tf_op jit(solution)/shard_map/back/pallas_call | solution.py:411
  78.8 0.6 copy.14
  (4 shorter events, 0.1 us)
Async XLA Ops:
  0.0 2.0 %copy-start = (bf16[1024,512]{1,0:T(8,128)(2,1)S(1)}, bf16[1024,512]{1,0:T(8,128)(2,1)}, u32[]{:S(2)}) copy-start(bf16[1024,512]{1,0:T(8,128)(2,1)} %constant.38.clone.tlow_hbm) | copy-start | bytes 3145732
  2.0 1.2 %copy-start.1 = (bf16[1024,512]{1,0:T(8,128)(2,1)S(1)}, bf16[1024,512]{1,0:T(8,128)(2,1)}, u32[]{:S(2)}) copy-start(bf16[1024,512]{1,0:T(8,128)(2,1)} %constant.37.clone.thigh_hbm) | copy-start | bytes 3145732
  3.3 1.0 %copy-start.2 = (f32[2,16,32,128]{3,2,1,0:T(8,128)S(1)}, f32[2,16,32,128]{3,2,1,0:T(8,128)}, u32[]{:S(2)}) copy-start(f32[2,16,32,128]{3,2,1,0:T(8,128)} %x_ref.1) | copy-start | bytes 1572868
  4.3 0.9 %copy-start.3 = (bf16[256,256]{1,0:T(8,128)(2,1)S(1)}, bf16[256,256]{1,0:T(8,128)(2,1)}, u32[]{:S(2)}) copy-start(bf16[256,256]{1,0:T(8,128)(2,1)} %constant.36.clone.clow_ref) | copy-start | bytes 393220
  5.2 0.9 %copy-start.4 = (bf16[256,256]{1,0:T(8,128)(2,1)S(1)}, bf16[256,256]{1,0:T(8,128)(2,1)}, u32[]{:S(2)}) copy-start(bf16[256,256]{1,0:T(8,128)(2,1)} %constant.35.clone.chigh_ref) | copy-start | bytes 393220

commit v3 on v1

v3 whole, which is shorter than its diff:
```python
import math

import jax
import jax.numpy as jnp
import ml_dtypes
import numpy as np
from jax import lax
from jax.experimental import pallas as pl
from jax.experimental.pallas import tpu as pltpu
from jax.sharding import Mesh
from jax.sharding import PartitionSpec as P

CHANNELS = 128
BLOCKS = 512
ALPHAS = 64
SHIFTS = 8
FLOOR = 0.1
F32 = jnp.float32
BF16 = jnp.bfloat16
VMEM = pl.BlockSpec(memory_space=pltpu.VMEM)


def halves(table):
    high = table.astype(ml_dtypes.bfloat16)
    low = (table - high.astype(np.float64)).astype(ml_dtypes.bfloat16)
    return np.stack([high, low])


def channel_table():
    n = np.arange(CHANNELS)
    window = 0.5 - 0.5 * np.cos(2 * np.pi * n / CHANNELS)
    angle = 2 * np.pi * (n[:, None] * n[None, :] % CHANNELS) / CHANNELS
    cosine = window[:, None] * np.cos(angle) / math.sqrt(CHANNELS)
    sine = window[:, None] * np.sin(angle) / math.sqrt(CHANNELS)
    return halves(np.block([[cosine, -sine], [sine, cosine]]))


def block_table():
    n = np.arange(BLOCKS).reshape(16, 4, 8).transpose(1, 0, 2).reshape(-1)
    angle = 2 * np.pi * (n[:, None] * n[None, :] % BLOCKS) / BLOCKS
    return halves(np.concatenate([np.cos(angle), np.sin(angle)], 0) / math.sqrt(BLOCKS))


def split(x):
    high = x.astype(BF16)
    return high, (x - high.astype(F32)).astype(BF16)


def dot3(a, b, dims):
    def one(u, v):
        return lax.dot_general(u, v, (dims, ((), ())), preferred_element_type=F32)

    rows = a[0].shape[0]
    top = one(jnp.concatenate(a, 0), b[0])
    return top[:rows] + (top[rows:] + one(a[0], b[1]))


def lane_block(shape, width):
    return lax.broadcasted_iota(jnp.int32, shape, len(shape) - 1) // width % 2


def swap_blocks(tiles):
    tiles = list(tiles)
    for bit in (1, 2, 4, 8):
        width = 8 * bit
        upper = lane_block(tiles[0].shape, width) == 1
        for i in range(16):
            if i & bit:
                continue
            a, b = tiles[i], tiles[i | bit]
            axis = a.ndim - 1
            tiles[i] = jnp.where(upper, pltpu.roll(b, width, axis), a)
            tiles[i | bit] = jnp.where(upper, b, pltpu.roll(a, 128 - width, axis))
    return tiles


def remote(src, dst, send, recv, **where):
    return pltpu.make_async_remote_copy(
        src_ref=src,
        dst_ref=dst,
        send_sem=send,
        recv_sem=recv,
        device_id=where,
        device_id_type=pl.DeviceIdType.MESH,
    )


def phase_rows(bins_ref, offsets_ref, first):
    row = lax.broadcasted_iota(jnp.int32, (ALPHAS, ALPHAS), 0)
    same = row == lax.broadcasted_iota(jnp.int32, (ALPHAS, ALPHAS), 1)

    def column(ref):
        return jnp.sum(jnp.where(same, ref[...].astype(F32), 0.0), 1, keepdims=True)

    lane = lax.broadcasted_iota(jnp.int32, (ALPHAS, 256), 1)
    turns = column(bins_ref).astype(jnp.int32) * (first + lane // 8) % BLOCKS
    angle = turns.astype(F32) * (2.0 * math.pi / BLOCKS)
    chosen = column(offsets_ref).astype(jnp.int32) == lane % 8
    both = [jnp.where(chosen, f(angle) * (1.0 / 256.0), 0.0) for f in (jnp.cos, jnp.sin)]
    return split(jnp.concatenate(both, 0))


def kernel(
    x_hbm, bins_ref, offsets_ref, ctable_hbm, table_hbm, out_ref,
    x_ref, ctable_ref, table_ref, mid_ref, made_ref, got_ref, back_ref, land_ref,
    right_ref, other_ref, phase_ref, high_ref, low_ref, part_ref, pair_ref, sum_ref, all_ref, res_ref,
    load_sem, send1, recv1, send2, recv2, sendx, recvx, sendf, recvf, sendz, recvz,
    sendp, recvp, sends, recvs,
):
    chan, x, z = lax.axis_index("chan"), lax.axis_index("x"), lax.axis_index("z")
    core, place = lax.rem(chan, 2), chan // 2
    mate = chan + 1 - 2 * core
    after, before = lax.rem(x + 1, 4), lax.rem(x + 3, 4)

    barrier = pltpu.get_barrier_semaphore()
    peers = [{"chan": lax.rem(chan + o, 16)} for o in range(1, 16)]
    peers += [{"x": after}, {"x": before}]
    peers += [{"z": 1 - z, "chan": lax.rem(place + o, 8) * 2 + core} for o in range(8)]
    for where in peers:
        pl.semaphore_signal(barrier, device_id=where, device_id_type=pl.DeviceIdType.MESH)
    loads = [
        pltpu.make_async_copy(src, dst, load_sem.at[i])
        for i, (src, dst) in enumerate(
            [(x_hbm, x_ref), (ctable_hbm, ctable_ref), (table_hbm, table_ref)]
        )
    ]
    for load in loads:
        load.start()

    loads[0].wait()
    loads[1].wait()
    both = jnp.concatenate([x_ref[0].reshape(512, 128), x_ref[1].reshape(512, 128)], 1)
    mid_ref[...] = dot3(split(both), (ctable_ref[0], ctable_ref[1]), ((1,), (0,)))
    for c in range(2):
        for mc in range(4):
            tiles = [
                mid_ref[s * 32 + mc * 8 : s * 32 + mc * 8 + 8, c * 128 : c * 128 + 128]
                for s in range(16)
            ]
            for dest, tile in enumerate(swap_blocks(tiles)):
                made_ref[dest, mc, c] = tile
    pl.semaphore_wait(barrier, len(peers))

    def first_way(o, incoming):
        peer = lax.rem(chan + o, 16)
        at = peer if incoming else chan
        return remote(made_ref.at[peer], got_ref.at[at], send1.at[o], recv1.at[at], chan=peer)

    @pl.loop(1, 16)
    def _(o):
        first_way(o, False).start()

    got_ref[chan] = made_ref[chan]
    phase_ref[0], phase_ref[1] = phase_rows(bins_ref, offsets_ref, chan * 32)
    loads[2].wait()

    @pl.loop(1, 16)
    def _(o):
        first_way(o, True).wait_recv()

    def gathered(c):
        return jnp.concatenate([got_ref[:, mc, c].reshape(128, 128) for mc in range(4)], 0)

    u = dot3(
        (table_ref[0], table_ref[1]),
        split(jnp.concatenate([gathered(0), gathered(1)], 1)),
        ((1,), (0,)),
    )
    real = u[:BLOCKS, :128] + u[BLOCKS:, 128:]
    imag = u[:BLOCKS, 128:] - u[BLOCKS:, :128]
    scale = 1.0 / jnp.sqrt(real * real + imag * imag + FLOOR)
    white = split(jnp.concatenate([real * scale, imag * scale], 1))

    def second_way(o, mc, incoming):
        peer = lax.rem(chan + o, 16)
        at = peer if incoming else chan
        return remote(
            back_ref.at[peer, mc], land_ref.at[at, mc], send2.at[mc, o], recv2.at[mc, at], chan=peer
        )

    for mc in range(4):
        rows = [
            jnp.concatenate([table_ref[i, at : at + 128, :] for at in (mc * 128, BLOCKS + mc * 128)], 0)
            for i in range(2)
        ]
        u = dot3(rows, white, ((1,), (0,)))
        back_ref[:, mc, 0] = (u[:128, :128] - u[128:, 128:]).reshape(16, 8, 128)
        back_ref[:, mc, 1] = (u[:128, 128:] + u[128:, :128]).reshape(16, 8, 128)

        @pl.loop(1, 16)
        def _(o, mc=mc):
            second_way(o, mc, False).start()

        land_ref[chan, mc] = back_ref[chan, mc]

    def to_x(mc, way, incoming=False):
        peer = (after, before)[way ^ incoming]
        at = peer if incoming else x
        return remote(
            right_ref.at[x, mc], right_ref.at[at, mc], sendx.at[way, mc], recvx.at[way, mc], x=peer
        )

    def passed(mc, incoming=False):
        source, peer = (before, after) if mc % 2 == 0 else (after, before)
        at = lax.rem(x + 2, 4) if incoming else source
        return remote(right_ref.at[source, mc], right_ref.at[at, mc], sendf.at[mc], recvf.at[mc], x=peer)

    def to_z(mc):
        return remote(right_ref.at[x, mc], other_ref.at[mc], sendz.at[mc], recvz.at[mc], z=1 - z)

    def turn(mc):
        @pl.loop(1, 16)
        def _(o):
            second_way(o, mc, True).wait_recv()

        for c in range(2):
            tiles = [land_ref[i, mc, c] for i in range(16)]
            for s, tile in enumerate(swap_blocks(tiles)):
                right_ref[x, mc, s, c] = tile
        to_x(mc, 0).start()
        to_x(mc, 1).start()
        to_z(mc).start()

    def forward(mc):
        to_x(mc, mc % 2, True).wait_recv()
        passed(mc).start()

    def product(mc, r):
        left = []
        for c in range(2):
            rows = []
            for a in range(32):
                if a < 16:
                    row = right_ref[x, mc, a, c, pl.ds(r, 1), :]
                else:
                    row = other_ref[mc, a - 16, c, pl.ds(r, 1), :]
                rows.append(pltpu.roll(jnp.broadcast_to(row, (8, 128)), 0, 1, stride=1, stride_axis=0))
            left.append(jnp.concatenate(rows, 0))
        left = split(jnp.concatenate(left, 1))
        rows = []
        for i in range(4):
            tall = right_ref.at[i, mc].reshape(256, 128)
            real, imag = (tall[pl.ds(r + c * 8, 16, stride=16), :] for c in range(2))
            rows.append(jnp.concatenate([real, imag], 1))
            rows.append(jnp.concatenate([-imag, real], 1))
        right = split(jnp.concatenate(rows, 0))
        return dot3(left, right, ((1,), (1,))).reshape(32, 8, 128)

    def products(mc):
        to_x(mc, 1 - mc % 2, True).wait_recv()
        to_z(mc).wait_recv()
        passed(mc, True).wait_recv()

        def step(i, carry):
            for half in range(2):
                r = i * 4 + half * 2
                tiles = jnp.concatenate([product(mc, r), product(mc, r + 1)], 1)
                rows = pl.ds(pl.multiple_of(mc * 64 + r * 8, 16), 16)
                high_ref[:, rows, :], low_ref[:, rows, :] = split(tiles)
            return carry

        lax.fori_loop(0, 2, step, 0)

    turn(0)
    turn(1)
    forward(0)
    turn(2)
    forward(1)
    turn(3)
    forward(2)
    products(0)
    forward(3)
    products(1)
    products(2)
    products(3)

    low = lax.broadcasted_iota(jnp.int32, (8, 128), 0) < 4

    def one_pair(half, pair):
        a = half * 16 + pair * 2
        both = tuple(jnp.concatenate([ref[a], ref[a + 1]], 1) for ref in (high_ref, low_ref))
        t = dot3((phase_ref[0], phase_ref[1]), both, ((1,), (0,)))
        gs = []
        for i in range(2):
            cosine, sine = t[:64, i * 128 : i * 128 + 128], t[64:, i * 128 : i * 128 + 128]
            odd = lane_block(sine.shape, 16) == 1
            gs.append(cosine + jnp.where(odd, -pltpu.roll(sine, 16, 1), pltpu.roll(sine, 112, 1)))
        row = pl.ds(pl.multiple_of(pair * 8, 8), 8)
        for t8 in range(8):
            a0, a1 = (g[t8 * 8 : t8 * 8 + 8] for g in gs)
            part_ref[0, half, t8, row, :] = jnp.where(low, a0, pltpu.roll(a1, 4, 0))
            part_ref[1, half, t8, row, :] = jnp.where(low, pltpu.roll(a0, 4, 0), a1)

    def to_mate(half, piece):
        rows = pl.ds(piece * 32, 32)
        at = half * 2 + piece
        return remote(
            part_ref.at[1 - core, half, :, rows], pair_ref.at[half, :, rows],
            sendp.at[at], recvp.at[at], chan=mate,
        )

    def spread(piece, o, incoming=False):
        peer_z, peer = lax.rem(z + o // 8, 2), lax.rem(place + lax.rem(o, 8), 8)
        rows = pl.ds(piece * 32, 32)
        at_z, at = (peer_z, peer) if incoming else (z, place)
        return remote(
            sum_ref.at[o // 8, peer, rows], all_ref.at[at_z, at, rows],
            sends.at[piece, o], recvs.at[piece, at_z, at],
            z=peer_z, chan=peer * 2 + core,
        )

    def add_and_send(half, piece):
        to_mate(half, piece).wait_recv()
        rows = pl.ds(piece * 32, 32)
        sum_ref[half, :, rows] = part_ref[core, half, :, rows] + pair_ref[half, :, rows]

        @pl.loop(8 if half else 1, 16 if half else 8)
        def _(o):
            spread(piece, o).start()

        if not half:
            all_ref[z, place, rows] = sum_ref[0, place, rows]

    order = [(1, 0), (1, 1), (0, 0), (0, 1)]
    for i, (half, piece) in enumerate(order):

        def step(p, carry, half=half, piece=piece):
            one_pair(half, piece * 4 + p * 2)
            one_pair(half, piece * 4 + p * 2 + 1)
            return carry

        lax.fori_loop(0, 2, step, 0)
        to_mate(half, piece).start()
        if i:
            add_and_send(*order[i - 1])
    add_and_send(*order[3])

    @pl.loop(1, 16)
    def _(o):
        for piece in range(2):
            spread(piece, o, True).wait_recv()

    lo, hi = (jnp.sum(all_ref[h], axis=0) for h in range(2))
    odd = lane_block(lo.shape, 16) == 1
    res_ref[0] = jnp.where(odd, pltpu.roll(hi, 16, 1), lo)
    res_ref[1] = jnp.where(odd, hi, pltpu.roll(lo, 112, 1))
    for j in range(4):
        for c in range(2):
            out_ref[j, c] = res_ref[c, pl.ds(j, 16, stride=4), :]

    @pl.loop(1, 16)
    def _(o):
        first_way(o, False).wait_send()
        for mc in range(4):
            second_way(o, mc, False).wait_send()
        for piece in range(2):
            spread(piece, o).wait_send()

    for mc in range(4):
        to_x(mc, 0).wait_send()
        to_x(mc, 1).wait_send()
        to_z(mc).wait_send()
        passed(mc).wait_send()
        to_mate(mc // 2, mc % 2).wait_send()


DMA = pltpu.SemaphoreType.DMA
HBM = pl.BlockSpec(memory_space=pltpu.HBM)


def on_device(samples, bins, offsets):
    chunk = pltpu.VMEM((16, 4, 2, 8, 128), F32)
    eighths = pltpu.VMEM((2, 8, 64, 128), F32)
    return pl.pallas_call(
        kernel,
        out_shape=jax.ShapeDtypeStruct((4, 2, 16, 128), F32),
        in_specs=[HBM, VMEM, VMEM, HBM, HBM],
        out_specs=VMEM,
        scratch_shapes=[
            pltpu.VMEM((2, 16, 32, 128), F32),
            pltpu.VMEM((2, 256, 256), BF16),
            pltpu.VMEM((2, 2 * BLOCKS, BLOCKS), BF16),
            pltpu.VMEM((512, 256), F32),
            chunk, chunk, chunk, chunk,
            pltpu.VMEM((4, 4, 16, 2, 8, 128), F32),
            pltpu.VMEM((4, 16, 2, 8, 128), F32),
            pltpu.VMEM((2, 128, 256), BF16),
            pltpu.VMEM((32, 256, 128), BF16),
            pltpu.VMEM((32, 256, 128), BF16),
            pltpu.VMEM((2, 2, 8, 64, 128), F32),
            eighths, eighths, eighths,
            pltpu.VMEM((2, 64, 128), F32),
            DMA((3,)), DMA((16,)), DMA((16,)), DMA((4, 16)), DMA((4, 16)),
            DMA((2, 4)), DMA((2, 4)), DMA((4,)), DMA((4,)), DMA((4,)), DMA((4,)),
            DMA((4,)), DMA((4,)), DMA((2, 16)), DMA((2, 2, 8)),
        ],
        compiler_params=pltpu.CompilerParams(
            vmem_limit_bytes=48 * 2**20, collective_id=0, has_side_effects=True
        ),
        name="coherence",
    )(samples, bins.reshape(1, -1), offsets.reshape(1, -1), channel_table(), block_table())


def solution(mesh):
    finer = Mesh(mesh.devices.reshape(4, 2, mesh.shape["chan"]), ("x", "z", "chan"))
    sensor = ("x", "z")
    return jax.shard_map(
        on_device,
        mesh=finer,
        in_specs=(P(None, sensor, "chan", None), P(), P()),
        out_specs=P("chan", None, sensor, None),
        check_vma=False,
    )
```

time: 140 us -> 66.8 us (0.48); the launches traced: 138 us -> 66.6 us
  blocking collectives: 59.8 us -> 0 us
  Pallas kernels: 26.5 us -> 61 us
  waiting for transfers between devices: 27.9 us -> 0 us
  between operations: 13.6 us -> 0.01 us
  other arithmetic: 1.95 us -> 0 us
  local copies, waits for them, and re-layouts: 7.36 us -> 5.52 us
    all_to_all x3 -> x0, blocking collectives: 59.8 us -> none  [the longest x1 24.4 us: on_device(): lax.all_to_all(part[:, None], 'chan', 0, 0, tiled=True)]
    pallas_call x4 -> x1, Pallas kernels: 26.5 us -> 61 us  [on_device(): pl.pallas_call(kernel, out_shape=jax.ShapeDtypeStruct((4, 2, 16, 128), F3...]
    all_gather x1 -> x0, waiting for transfers between devices: 14 us -> none  [on_device(): right = lax.all_gather(own, 'x', axis=0, tiled=True)]
    ppermute x2 -> x0, waiting for transfers between devices: 13.9 us -> none  [the longest x1 11.5 us: on_device(): other = lax.ppermute(own, 'z', [(0, 1), (1, 0)])]
    unnamed x16 -> x11, local copies, waits for them, and re-layouts: 4.61 us -> 5.52 us
  transfers between devices with their start and end apart: 3 -> 0, of which waited for: 3 -> 0; matrix products, arithmetic and copies ran while one was open for 1% -> 0% of each run, Pallas kernels for 0% -> 0%
where the time goes in v3:
time: 66.8 us; the launch traced here: 66.6 us
  Pallas kernels  61 us (91%)
  local copies, waits for them, and re-layouts  5.52 us (8%)
    pallas_call x1, Pallas kernels, on_device(): pl.pallas_call(kernel, out_shape=jax.ShapeDtypeStruct((4, 2, 16, 128), F3...  61 us
    unnamed x11, local copies, waits for them, and re-layouts  5.52 us

profile of v3, /device:TPU:1, one launch (start us, length us, event | category | flops | bytes accessed | tf_op | source)
XLA Modules:
  0.0 66.6 jit_solution(3324149632296984586)
XLA Ops:
  0.0 0.0 copy-start
  0.0 1.6 %copy-done = bf16[2,1024,512]{2,1,0:T(8,128)(2,1)S(1)} copy-done((bf16[2,1024,512]{2,1,0:T(8,128)(2,1)S(1)}, bf16[2,1024,512]{2,1,0:T(8,128)(2,1)}, u32[]{:S(2)}) %copy-start) | copy-done | bytes 2097176
  1.6 0.0 copy-start.1
  1.6 1.0 %copy-done.1 = f32[2,16,32,128]{3,2,1,0:T(8,128)S(1)} copy-done((f32[2,16,32,128]{3,2,1,0:T(8,128)S(1)}, f32[2,16,32,128]{3,2,1,0:T(8,128)}, u32[]{:S(2)}) %copy-start.1) | copy-done | bytes 524312
  2.6 0.0 copy-start.2
  2.6 0.9 %copy-done.2 = bf16[2,256,256]{2,1,0:T(8,128)(2,1)S(1)} copy-done((bf16[2,256,256]{2,1,0:T(8,128)(2,1)S(1)}, bf16[2,256,256]{2,1,0:T(8,128)(2,1)}, u32[]{:S(2)}) %copy-start.2) | copy-done | bytes 262168
  3.6 0.0 copy-start.3
  3.6 0.7 copy-done.3
  4.2 0.0 copy-start.4
  4.2 0.7 copy-done.4
  4.9 61.0 %coherence.1 = f32[4,2,16,128]{3,2,1,0:T(8,128)S(1)} custom-call(f32[2,16,32,128]{3,2,1,0:T(8,128)S(1)} %copy-done.1, s32[1,64]{1,0:T(1,128)S(1)} %bitcast.2, s32[1,64]{1,0:T(1,128)S(1)} %bitcast.3, bf16[2,256,256]{2,1,0:T(8,128)(2,1)S(1)} %copy-done.2, bf16[2,1024,512]{2,1,0:T(8,128)(2,1)S(1)} %copy-done), custom_call_target="tpu_custom_call" | custom-call | tf_op jit(solution)/shard_map/coherence/pallas_call | solution.py:374
  65.9 0.6 copy.7
Async XLA Ops:
  0.0 1.6 %copy-start = (bf16[2,1024,512]{2,1,0:T(8,128)(2,1)S(1)}, bf16[2,1024,512]{2,1,0:T(8,128)(2,1)}, u32[]{:S(2)}) copy-start(bf16[2,1024,512]{2,1,0:T(8,128)(2,1)} %constant.5.clone.table_hbm) | copy-start | bytes 6291460
  1.6 1.0 %copy-start.1 = (f32[2,16,32,128]{3,2,1,0:T(8,128)S(1)}, f32[2,16,32,128]{3,2,1,0:T(8,128)}, u32[]{:S(2)}) copy-start(f32[2,16,32,128]{3,2,1,0:T(8,128)} %x_hbm.1) | copy-start | bytes 1572868
  2.6 0.9 %copy-start.2 = (bf16[2,256,256]{2,1,0:T(8,128)(2,1)S(1)}, bf16[2,256,256]{2,1,0:T(8,128)(2,1)}, u32[]{:S(2)}) copy-start(bf16[2,256,256]{2,1,0:T(8,128)(2,1)} %constant.4.clone.ctable_hbm) | copy-start | bytes 786436
  3.6 0.7 copy-start.3
  4.2 0.7 copy-start.4

commit v4 on v3

--- a/solution.py
+++ b/solution.py
@@ -18,6 +18,7 @@
 F32 = jnp.float32
 BF16 = jnp.bfloat16
 VMEM = pl.BlockSpec(memory_space=pltpu.VMEM)
+HBM = pl.BlockSpec(memory_space=pltpu.HBM)
 
 
 def halves(table):
@@ -101,8 +102,8 @@
 
 
 def kernel(
-    x_hbm, bins_ref, offsets_ref, ctable_hbm, table_hbm, out_ref,
-    x_ref, ctable_ref, table_ref, mid_ref, made_ref, got_ref, back_ref, land_ref,
+    x_hbm, bins_hbm, offsets_hbm, ctable_hbm, table_hbm, out_ref,
+    bins_ref, offsets_ref, x_ref, ctable_ref, table_ref, mid_ref, made_ref, got_ref, back_ref, land_ref,
     right_ref, other_ref, phase_ref, high_ref, low_ref, part_ref, pair_ref, sum_ref, all_ref, res_ref,
     load_sem, send1, recv1, send2, recv2, sendx, recvx, sendf, recvf, sendz, recvz,
     sendp, recvp, sends, recvs,
@@ -121,7 +122,13 @@
     loads = [
         pltpu.make_async_copy(src, dst, load_sem.at[i])
         for i, (src, dst) in enumerate(
-            [(x_hbm, x_ref), (ctable_hbm, ctable_ref), (table_hbm, table_ref)]
+            [
+                (x_hbm, x_ref),
+                (ctable_hbm, ctable_ref),
+                (table_hbm, table_ref),
+                (bins_hbm, bins_ref),
+                (offsets_hbm, offsets_ref),
+            ]
         )
     ]
     for load in loads:
@@ -151,6 +158,8 @@
         first_way(o, False).start()
 
     got_ref[chan] = made_ref[chan]
+    loads[3].wait()
+    loads[4].wait()
     phase_ref[0], phase_ref[1] = phase_rows(bins_ref, offsets_ref, chan * 32)
     loads[2].wait()
 
@@ -365,7 +374,6 @@
 
 
 DMA = pltpu.SemaphoreType.DMA
-HBM = pl.BlockSpec(memory_space=pltpu.HBM)
 
 
 def on_device(samples, bins, offsets):
@@ -374,9 +382,11 @@
     return pl.pallas_call(
         kernel,
         out_shape=jax.ShapeDtypeStruct((4, 2, 16, 128), F32),
-        in_specs=[HBM, VMEM, VMEM, HBM, HBM],
+        in_specs=[HBM] * 5,
         out_specs=VMEM,
         scratch_shapes=[
+            pltpu.VMEM((1, ALPHAS), jnp.int32),
+            pltpu.VMEM((1, ALPHAS), jnp.int32),
             pltpu.VMEM((2, 16, 32, 128), F32),
             pltpu.VMEM((2, 256, 256), BF16),
             pltpu.VMEM((2, 2 * BLOCKS, BLOCKS), BF16),
@@ -390,12 +400,12 @@
             pltpu.VMEM((2, 2, 8, 64, 128), F32),
             eighths, eighths, eighths,
             pltpu.VMEM((2, 64, 128), F32),
-            DMA((3,)), DMA((16,)), DMA((16,)), DMA((4, 16)), DMA((4, 16)),
+            DMA((5,)), DMA((16,)), DMA((16,)), DMA((4, 16)), DMA((4, 16)),
             DMA((2, 4)), DMA((2, 4)), DMA((4,)), DMA((4,)), DMA((4,)), DMA((4,)),
             DMA((4,)), DMA((4,)), DMA((2, 16)), DMA((2, 2, 8)),
         ],
         compiler_params=pltpu.CompilerParams(
-            vmem_limit_bytes=48 * 2**20, collective_id=0, has_side_effects=True
+            vmem_limit_bytes=60 * 2**20, collective_id=0, has_side_effects=True
         ),
         name="coherence",
     )(samples, bins.reshape(1, -1), offsets.reshape(1, -1), channel_table(), block_table())

time: 66.8 us -> 63.3 us (0.948)
  local copies, waits for them, and re-layouts: 5.52 us -> 1.47 us
    unnamed x11 -> x1, local copies, waits for them, and re-layouts: 5.52 us -> 1.47 us
where the time goes in v4:
time: 63.3 us; the launch traced here: 63.1 us
  Pallas kernels  61.6 us (97%)
  local copies, waits for them, and re-layouts  1.47 us (2%)
    pallas_call x1, Pallas kernels, on_device(): pl.pallas_call(kernel, out_shape=jax.ShapeDtypeStruct((4, 2, 16, 128), F3...  61.6 us
    unnamed x1, local copies, waits for them, and re-layouts  1.47 us

profile of v4, /device:TPU:1, one launch (start us, length us, event | category | flops | bytes accessed | tf_op | source)
XLA Modules:
  0.0 63.1 jit_solution(18076896111405561486)
XLA Ops:
  0.0 61.6 %coherence.1 = f32[4,2,16,128]{3,2,1,0:T(8,128)} custom-call(f32[2,16,32,128]{3,2,1,0:T(8,128)} %x_hbm.1, s32[1,64]{1,0:T(1,128)} %bitcast.2, s32[1,64]{1,0:T(1,128)} %bitcast.3, bf16[2,256,256]{2,1,0:T(8,128)(2,1)} %constant.4.clone.ctable_hbm, bf16[2,1024,512]{2,1,0:T(8,128)(2,1)} %constant.5.clone.table_hbm), custom_call_target="tpu_custom_call" | custom-call | tf_op jit(solution)/shard_map/coherence/pallas_call | solution.py:382
  61.6 1.5 %copy.7 = f32[4,2,16,128]{3,2,1,0:T(8,128)} copy(f32[4,2,16,128]{3,2,1,0:T(8,128)} %coherence.1) | data formatting | bytes 131072

commit v5 on v4

--- a/solution.py
+++ b/solution.py
@@ -138,101 +138,105 @@
     loads[1].wait()
     both = jnp.concatenate([x_ref[0].reshape(512, 128), x_ref[1].reshape(512, 128)], 1)
     mid_ref[...] = dot3(split(both), (ctable_ref[0], ctable_ref[1]), ((1,), (0,)))
-    for c in range(2):
+
+    def tiles_of(h):
         for mc in range(4):
             tiles = [
                 mid_ref[s * 32 + mc * 8 : s * 32 + mc * 8 + 8, c * 128 : c * 128 + 128]
-                for s in range(16)
+                for c in range(2)
+                for s in range(h * 8, h * 8 + 8)
             ]
             for dest, tile in enumerate(swap_blocks(tiles)):
-                made_ref[dest, mc, c] = tile
-    pl.semaphore_wait(barrier, len(peers))
-
-    def first_way(o, incoming):
+                made_ref[h, dest, mc] = tile
+
+    def exchange(src, dst, send, recv, h, o, incoming):
         peer = lax.rem(chan + o, 16)
         at = peer if incoming else chan
-        return remote(made_ref.at[peer], got_ref.at[at], send1.at[o], recv1.at[at], chan=peer)
-
-    @pl.loop(1, 16)
-    def _(o):
-        first_way(o, False).start()
-
-    got_ref[chan] = made_ref[chan]
+        return remote(src.at[h, peer], dst.at[h, at], send.at[h, o], recv.at[h, at], chan=peer)
+
+    def first_way(h, o, incoming=False):
+        return exchange(made_ref, got_ref, send1, recv1, h, o, incoming)
+
+    def second_way(h, o, incoming=False):
+        return exchange(back_ref, land_ref, send2, recv2, h, o, incoming)
+
+    def send_all(way, h):
+        @pl.loop(1, 16)
+        def _(o):
+            way(h, o).start()
+
+    def wait_all(way, h):
+        @pl.loop(1, 16)
+        def _(o):
+            way(h, o, True).wait_recv()
+
+    tiles_of(0)
+    pl.semaphore_wait(barrier, len(peers))
+    send_all(first_way, 0)
+    tiles_of(1)
+    send_all(first_way, 1)
+    for h in range(2):
+        got_ref[h, chan] = made_ref[h, chan]
     loads[3].wait()
     loads[4].wait()
     phase_ref[0], phase_ref[1] = phase_rows(bins_ref, offsets_ref, chan * 32)
     loads[2].wait()
 
-    @pl.loop(1, 16)
-    def _(o):
-        first_way(o, True).wait_recv()
-
-    def gathered(c):
-        return jnp.concatenate([got_ref[:, mc, c].reshape(128, 128) for mc in range(4)], 0)
-
-    u = dot3(
-        (table_ref[0], table_ref[1]),
-        split(jnp.concatenate([gathered(0), gathered(1)], 1)),
-        ((1,), (0,)),
-    )
-    real = u[:BLOCKS, :128] + u[BLOCKS:, 128:]
-    imag = u[:BLOCKS, 128:] - u[BLOCKS:, :128]
-    scale = 1.0 / jnp.sqrt(real * real + imag * imag + FLOOR)
-    white = split(jnp.concatenate([real * scale, imag * scale], 1))
-
-    def second_way(o, mc, incoming):
-        peer = lax.rem(chan + o, 16)
-        at = peer if incoming else chan
-        return remote(
-            back_ref.at[peer, mc], land_ref.at[at, mc], send2.at[mc, o], recv2.at[mc, at], chan=peer
-        )
-
-    for mc in range(4):
-        rows = [
-            jnp.concatenate([table_ref[i, at : at + 128, :] for at in (mc * 128, BLOCKS + mc * 128)], 0)
-            for i in range(2)
-        ]
-        u = dot3(rows, white, ((1,), (0,)))
-        back_ref[:, mc, 0] = (u[:128, :128] - u[128:, 128:]).reshape(16, 8, 128)
-        back_ref[:, mc, 1] = (u[:128, 128:] + u[128:, :128]).reshape(16, 8, 128)
-
-        @pl.loop(1, 16)
-        def _(o, mc=mc):
-            second_way(o, mc, False).start()
-
-        land_ref[chan, mc] = back_ref[chan, mc]
-
-    def to_x(mc, way, incoming=False):
+    for h in range(2):
+        wait_all(first_way, h)
+        table = (table_ref[0], table_ref[1])
+        d = jnp.concatenate([got_ref[h, :, mc].reshape(128, 128) for mc in range(4)], 0)
+        u = dot3(table, split(d), ((1,), (0,)))
+        first_part = lax.broadcasted_iota(jnp.int32, (BLOCKS, 128), 1) < 64
+        turned = pltpu.roll(u[BLOCKS:], 64, 1)
+        spectra = u[:BLOCKS] + jnp.where(first_part, turned, -turned)
+        power = spectra * spectra
+        power = power + pltpu.roll(power, 64, 1)
+        white = spectra / jnp.sqrt(power + FLOOR)
+        u = dot3(table, split(white), ((1,), (0,)))
+        turned = pltpu.roll(u[BLOCKS:], 64, 1)
+        blocks = u[:BLOCKS] + jnp.where(first_part, -turned, turned)
+        for mc in range(4):
+            back_ref[h, :, mc] = blocks[mc * 128 : mc * 128 + 128].reshape(16, 8, 128)
+        send_all(second_way, h)
+        land_ref[h, chan] = back_ref[h, chan]
+
+    def eight(i, mc, h):
+        return right_ref.at[i, mc, pl.ds(h * 8, 8)]
+
+    def to_x(h, mc, way, incoming=False):
         peer = (after, before)[way ^ incoming]
         at = peer if incoming else x
         return remote(
-            right_ref.at[x, mc], right_ref.at[at, mc], sendx.at[way, mc], recvx.at[way, mc], x=peer
-        )
-
-    def passed(mc, incoming=False):
-        source, peer = (before, after) if mc % 2 == 0 else (after, before)
+            eight(x, mc, h), eight(at, mc, h), sendx.at[way, h, mc], recvx.at[way, h, mc], x=peer
+        )
+
+    def passed(h, mc, way, incoming=False):
+        source, peer = (before, after) if way == 0 else (after, before)
         at = lax.rem(x + 2, 4) if incoming else source
-        return remote(right_ref.at[source, mc], right_ref.at[at, mc], sendf.at[mc], recvf.at[mc], x=peer)
-
-    def to_z(mc):
-        return remote(right_ref.at[x, mc], other_ref.at[mc], sendz.at[mc], recvz.at[mc], z=1 - z)
-
-    def turn(mc):
-        @pl.loop(1, 16)
-        def _(o):
-            second_way(o, mc, True).wait_recv()
-
-        for c in range(2):
-            tiles = [land_ref[i, mc, c] for i in range(16)]
-            for s, tile in enumerate(swap_blocks(tiles)):
-                right_ref[x, mc, s, c] = tile
-        to_x(mc, 0).start()
-        to_x(mc, 1).start()
-        to_z(mc).start()
-
-    def forward(mc):
-        to_x(mc, mc % 2, True).wait_recv()
-        passed(mc).start()
+        four = pl.ds(h * 8 + way * 4, 4)
+        return remote(
+            right_ref.at[source, mc, four], right_ref.at[at, mc, four],
+            sendf.at[way, h, mc], recvf.at[way, h, mc], x=peer,
+        )
+
+    def to_z(h, mc):
+        return remote(
+            eight(x, mc, h), other_ref.at[mc, pl.ds(h * 8, 8)], sendz.at[h, mc], recvz.at[h, mc], z=1 - z
+        )
+
+    def turn(h, mc):
+        tiles = swap_blocks([land_ref[h, i, mc] for i in range(16)])
+        for i, tile in enumerate(tiles):
+            right_ref[x, mc, h * 8 + i % 8, i // 8] = tile
+        to_x(h, mc, 0).start()
+        to_x(h, mc, 1).start()
+        to_z(h, mc).start()
+
+    def forward(h, mc):
+        for way in range(2):
+            to_x(h, mc, way, True).wait_recv()
+            passed(h, mc, way).start()
 
     def product(mc, r):
         left = []
@@ -256,9 +260,10 @@
         return dot3(left, right, ((1,), (1,))).reshape(32, 8, 128)
 
     def products(mc):
-        to_x(mc, 1 - mc % 2, True).wait_recv()
-        to_z(mc).wait_recv()
-        passed(mc, True).wait_recv()
+        for h in range(2):
+            to_z(h, mc).wait_recv()
+            for way in range(2):
+                passed(h, mc, way, True).wait_recv()
 
         def step(i, carry):
             for half in range(2):
@@ -270,18 +275,17 @@
 
         lax.fori_loop(0, 2, step, 0)
 
-    turn(0)
-    turn(1)
-    forward(0)
-    turn(2)
-    forward(1)
-    turn(3)
-    forward(2)
-    products(0)
-    forward(3)
-    products(1)
-    products(2)
-    products(3)
+    wait_all(second_way, 0)
+    for mc in range(4):
+        turn(0, mc)
+    wait_all(second_way, 1)
+    for mc in range(4):
+        turn(1, mc)
+        forward(0, mc)
+    for mc in range(4):
+        forward(1, mc)
+    for mc in range(4):
+        products(mc)
 
     low = lax.broadcasted_iota(jnp.int32, (8, 128), 0) < 4
 
@@ -294,7 +298,7 @@
             cosine, sine = t[:64, i * 128 : i * 128 + 128], t[64:, i * 128 : i * 128 + 128]
             odd = lane_block(sine.shape, 16) == 1
             gs.append(cosine + jnp.where(odd, -pltpu.roll(sine, 16, 1), pltpu.roll(sine, 112, 1)))
-        row = pl.ds(pl.multiple_of(pair * 8, 8), 8)
+        row = pl.ds(pair * 8, 8)
         for t8 in range(8):
             a0, a1 = (g[t8 * 8 : t8 * 8 + 8] for g in gs)
             part_ref[0, half, t8, row, :] = jnp.where(low, a0, pltpu.roll(a1, 4, 0))
@@ -333,12 +337,8 @@
     order = [(1, 0), (1, 1), (0, 0), (0, 1)]
     for i, (half, piece) in enumerate(order):
 
-        def step(p, carry, half=half, piece=piece):
-            one_pair(half, piece * 4 + p * 2)
-            one_pair(half, piece * 4 + p * 2 + 1)
-            return carry
-
-        lax.fori_loop(0, 2, step, 0)
+        for pair in range(piece * 4, piece * 4 + 4):
+            one_pair(half, pair)
         to_mate(half, piece).start()
         if i:
             add_and_send(*order[i - 1])
@@ -359,17 +359,18 @@
 
     @pl.loop(1, 16)
     def _(o):
-        first_way(o, False).wait_send()
-        for mc in range(4):
-            second_way(o, mc, False).wait_send()
+        for h in range(2):
+            first_way(h, o).wait_send()
+            second_way(h, o).wait_send()
         for piece in range(2):
             spread(piece, o).wait_send()
 
     for mc in range(4):
-        to_x(mc, 0).wait_send()
-        to_x(mc, 1).wait_send()
-        to_z(mc).wait_send()
-        passed(mc).wait_send()
+        for h in range(2):
+            for way in range(2):
+                to_x(h, mc, way).wait_send()
+                passed(h, mc, way).wait_send()
+            to_z(h, mc).wait_send()
         to_mate(mc // 2, mc % 2).wait_send()
 
 
@@ -377,7 +378,7 @@
 
 
 def on_device(samples, bins, offsets):
-    chunk = pltpu.VMEM((16, 4, 2, 8, 128), F32)
+    chunk = pltpu.VMEM((2, 16, 4, 8, 128), F32)
     eighths = pltpu.VMEM((2, 8, 64, 128), F32)
     return pl.pallas_call(
         kernel,
@@ -400,8 +401,8 @@
             pltpu.VMEM((2, 2, 8, 64, 128), F32),
             eighths, eighths, eighths,
             pltpu.VMEM((2, 64, 128), F32),
-            DMA((5,)), DMA((16,)), DMA((16,)), DMA((4, 16)), DMA((4, 16)),
-            DMA((2, 4)), DMA((2, 4)), DMA((4,)), DMA((4,)), DMA((4,)), DMA((4,)),
+            DMA((5,)), DMA((2, 16)), DMA((2, 16)), DMA((2, 16)), DMA((2, 16)),
+            DMA((2, 2, 4)), DMA((2, 2, 4)), DMA((2, 2, 4)), DMA((2, 2, 4)), DMA((2, 4)), DMA((2, 4)),
             DMA((4,)), DMA((4,)), DMA((2, 16)), DMA((2, 2, 8)),
         ],
         compiler_params=pltpu.CompilerParams(

time: 63.3 us -> 65 us (1.027)
  Pallas kernels: 61.6 us -> 63.3 us
    pallas_call x1, Pallas kernels: 61.6 us -> 63.3 us  [on_device(): pl.pallas_call(kernel, out_shape=jax.ShapeDtypeStruct((4, 2, 16, 128), F3...]
where the time goes in v5:
time: 65 us; the launch traced here: 64.8 us
  Pallas kernels  63.3 us (97%)
  local copies, waits for them, and re-layouts  1.47 us (2%)
    pallas_call x1, Pallas kernels, on_device(): pl.pallas_call(kernel, out_shape=jax.ShapeDtypeStruct((4, 2, 16, 128), F3...  63.3 us
    unnamed x1, local copies, waits for them, and re-layouts  1.47 us

profile of v5, /device:TPU:1, one launch (start us, length us, event | category | flops | bytes accessed | tf_op | source)
XLA Modules:
  0.0 64.8 jit_solution(6788056283430578981)
XLA Ops:
  0.0 63.3 %coherence.1 = f32[4,2,16,128]{3,2,1,0:T(8,128)} custom-call(f32[2,16,32,128]{3,2,1,0:T(8,128)} %x_hbm.1, s32[1,64]{1,0:T(1,128)} %bitcast.2, s32[1,64]{1,0:T(1,128)} %bitcast.3, bf16[2,256,256]{2,1,0:T(8,128)(2,1)} %constant.4.clone.ctable_hbm, bf16[2,1024,512]{2,1,0:T(8,128)(2,1)} %constant.5.clone.table_hbm), custom_call_target="tpu_custom_call" | custom-call | tf_op jit(solution)/shard_map/coherence/pallas_call | solution.py:383
  63.3 1.5 %copy.7 = f32[4,2,16,128]{3,2,1,0:T(8,128)} copy(f32[4,2,16,128]{3,2,1,0:T(8,128)} %coherence.1) | data formatting | bytes 131072

commit v6 on v4

--- a/solution.py
+++ b/solution.py
@@ -113,12 +113,6 @@
     mate = chan + 1 - 2 * core
     after, before = lax.rem(x + 1, 4), lax.rem(x + 3, 4)
 
-    barrier = pltpu.get_barrier_semaphore()
-    peers = [{"chan": lax.rem(chan + o, 16)} for o in range(1, 16)]
-    peers += [{"x": after}, {"x": before}]
-    peers += [{"z": 1 - z, "chan": lax.rem(place + o, 8) * 2 + core} for o in range(8)]
-    for where in peers:
-        pl.semaphore_signal(barrier, device_id=where, device_id_type=pl.DeviceIdType.MESH)
     loads = [
         pltpu.make_async_copy(src, dst, load_sem.at[i])
         for i, (src, dst) in enumerate(
@@ -134,6 +128,13 @@
     for load in loads:
         load.start()
 
+    barrier = pltpu.get_barrier_semaphore()
+    peers = [{"chan": lax.rem(chan + o, 16)} for o in range(1, 16)]
+    peers += [{"x": after}, {"x": before}]
+    peers += [{"z": 1 - z, "chan": lax.rem(place + o, 8) * 2 + core} for o in range(8)]
+    for where in peers:
+        pl.semaphore_signal(barrier, device_id=where, device_id_type=pl.DeviceIdType.MESH)
+
     loads[0].wait()
     loads[1].wait()
     both = jnp.concatenate([x_ref[0].reshape(512, 128), x_ref[1].reshape(512, 128)], 1)
@@ -148,14 +149,19 @@
                 made_ref[dest, mc, c] = tile
     pl.semaphore_wait(barrier, len(peers))
 
-    def first_way(o, incoming):
+    def exchange(src, dst, send, recv, o):
         peer = lax.rem(chan + o, 16)
-        at = peer if incoming else chan
-        return remote(made_ref.at[peer], got_ref.at[at], send1.at[o], recv1.at[at], chan=peer)
+        return remote(src.at[peer], dst.at[chan], send, recv, chan=peer)
+
+    def everyone(src, dst, send, recv):
+        most = pl.ds(0, 15)
+        return remote(src.at[most], dst.at[most], send, recv, chan=mate)
+
+    first = (made_ref, got_ref, send1, recv1)
 
     @pl.loop(1, 16)
     def _(o):
-        first_way(o, False).start()
+        exchange(*first, o).start()
 
     got_ref[chan] = made_ref[chan]
     loads[3].wait()
@@ -163,9 +169,7 @@
     phase_ref[0], phase_ref[1] = phase_rows(bins_ref, offsets_ref, chan * 32)
     loads[2].wait()
 
-    @pl.loop(1, 16)
-    def _(o):
-        first_way(o, True).wait_recv()
+    everyone(*first).wait_recv()
 
     def gathered(c):
         return jnp.concatenate([got_ref[:, mc, c].reshape(128, 128) for mc in range(4)], 0)
@@ -180,12 +184,8 @@
     scale = 1.0 / jnp.sqrt(real * real + imag * imag + FLOOR)
     white = split(jnp.concatenate([real * scale, imag * scale], 1))
 
-    def second_way(o, mc, incoming):
-        peer = lax.rem(chan + o, 16)
-        at = peer if incoming else chan
-        return remote(
-            back_ref.at[peer, mc], land_ref.at[at, mc], send2.at[mc, o], recv2.at[mc, at], chan=peer
-        )
+    def second(mc):
+        return back_ref.at[mc], land_ref.at[mc], send2.at[mc], recv2.at[mc]
 
     for mc in range(4):
         rows = [
@@ -193,14 +193,16 @@
             for i in range(2)
         ]
         u = dot3(rows, white, ((1,), (0,)))
-        back_ref[:, mc, 0] = (u[:128, :128] - u[128:, 128:]).reshape(16, 8, 128)
-        back_ref[:, mc, 1] = (u[:128, 128:] + u[128:, :128]).reshape(16, 8, 128)
+        back_ref[mc, :, 0] = (u[:128, :128] - u[128:, 128:]).reshape(16, 8, 128)
+        back_ref[mc, :, 1] = (u[:128, 128:] + u[128:, :128]).reshape(16, 8, 128)
+        if mc:
+            everyone(*second(mc - 1)).wait_send()
 
         @pl.loop(1, 16)
         def _(o, mc=mc):
-            second_way(o, mc, False).start()
-
-        land_ref[chan, mc] = back_ref[chan, mc]
+            exchange(*second(mc), o).start()
+
+        land_ref[mc, chan] = back_ref[mc, chan]
 
     def to_x(mc, way, incoming=False):
         peer = (after, before)[way ^ incoming]
@@ -218,12 +220,9 @@
         return remote(right_ref.at[x, mc], other_ref.at[mc], sendz.at[mc], recvz.at[mc], z=1 - z)
 
     def turn(mc):
-        @pl.loop(1, 16)
-        def _(o):
-            second_way(o, mc, True).wait_recv()
-
+        everyone(*second(mc)).wait_recv()
         for c in range(2):
-            tiles = [land_ref[i, mc, c] for i in range(16)]
+            tiles = [land_ref[mc, i, c] for i in range(16)]
             for s, tile in enumerate(swap_blocks(tiles)):
                 right_ref[x, mc, s, c] = tile
         to_x(mc, 0).start()
@@ -294,7 +293,7 @@
             cosine, sine = t[:64, i * 128 : i * 128 + 128], t[64:, i * 128 : i * 128 + 128]
             odd = lane_block(sine.shape, 16) == 1
             gs.append(cosine + jnp.where(odd, -pltpu.roll(sine, 16, 1), pltpu.roll(sine, 112, 1)))
-        row = pl.ds(pl.multiple_of(pair * 8, 8), 8)
+        row = pl.ds(pair * 8, 8)
         for t8 in range(8):
             a0, a1 = (g[t8 * 8 : t8 * 8 + 8] for g in gs)
             part_ref[0, half, t8, row, :] = jnp.where(low, a0, pltpu.roll(a1, 4, 0))
@@ -308,48 +307,39 @@
             sendp.at[at], recvp.at[at], chan=mate,
         )
 
-    def spread(piece, o, incoming=False):
+    def spread(piece, o):
         peer_z, peer = lax.rem(z + o // 8, 2), lax.rem(place + lax.rem(o, 8), 8)
         rows = pl.ds(piece * 32, 32)
-        at_z, at = (peer_z, peer) if incoming else (z, place)
         return remote(
-            sum_ref.at[o // 8, peer, rows], all_ref.at[at_z, at, rows],
-            sends.at[piece, o], recvs.at[piece, at_z, at],
-            z=peer_z, chan=peer * 2 + core,
+            sum_ref.at[o // 8 * 8 + peer, rows], all_ref.at[z * 8 + place, rows],
+            sends, recvs, z=peer_z, chan=peer * 2 + core,
         )
 
     def add_and_send(half, piece):
         to_mate(half, piece).wait_recv()
         rows = pl.ds(piece * 32, 32)
-        sum_ref[half, :, rows] = part_ref[core, half, :, rows] + pair_ref[half, :, rows]
+        sum_ref[half * 8 : half * 8 + 8, rows] = part_ref[core, half, :, rows] + pair_ref[half, :, rows]
 
         @pl.loop(8 if half else 1, 16 if half else 8)
         def _(o):
             spread(piece, o).start()
 
         if not half:
-            all_ref[z, place, rows] = sum_ref[0, place, rows]
+            all_ref[z * 8 + place, rows] = sum_ref[place, rows]
 
     order = [(1, 0), (1, 1), (0, 0), (0, 1)]
     for i, (half, piece) in enumerate(order):
 
-        def step(p, carry, half=half, piece=piece):
-            one_pair(half, piece * 4 + p * 2)
-            one_pair(half, piece * 4 + p * 2 + 1)
-            return carry
-
-        lax.fori_loop(0, 2, step, 0)
+        for pair in range(piece * 4, piece * 4 + 4):
+            one_pair(half, pair)
         to_mate(half, piece).start()
         if i:
             add_and_send(*order[i - 1])
     add_and_send(*order[3])
 
-    @pl.loop(1, 16)
-    def _(o):
-        for piece in range(2):
-            spread(piece, o, True).wait_recv()
-
-    lo, hi = (jnp.sum(all_ref[h], axis=0) for h in range(2))
+    last = (sum_ref, all_ref, sends, recvs)
+    everyone(*last).wait_recv()
+    lo, hi = (jnp.sum(all_ref[h * 8 : h * 8 + 8], axis=0) for h in range(2))
     odd = lane_block(lo.shape, 16) == 1
     res_ref[0] = jnp.where(odd, pltpu.roll(hi, 16, 1), lo)
     res_ref[1] = jnp.where(odd, hi, pltpu.roll(lo, 112, 1))
@@ -357,14 +347,8 @@
         for c in range(2):
             out_ref[j, c] = res_ref[c, pl.ds(j, 16, stride=4), :]
 
-    @pl.loop(1, 16)
-    def _(o):
-        first_way(o, False).wait_send()
-        for mc in range(4):
-            second_way(o, mc, False).wait_send()
-        for piece in range(2):
-            spread(piece, o).wait_send()
-
+    for group in (first, second(3), last):
+        everyone(*group).wait_send()
     for mc in range(4):
         to_x(mc, 0).wait_send()
         to_x(mc, 1).wait_send()
@@ -378,6 +362,8 @@
 
 def on_device(samples, bins, offsets):
     chunk = pltpu.VMEM((16, 4, 2, 8, 128), F32)
+    quarters = pltpu.VMEM((4, 16, 2, 8, 128), F32)
+    sixteen = pltpu.VMEM((16, 64, 128), F32)
     eighths = pltpu.VMEM((2, 8, 64, 128), F32)
     return pl.pallas_call(
         kernel,
@@ -391,18 +377,18 @@
             pltpu.VMEM((2, 256, 256), BF16),
             pltpu.VMEM((2, 2 * BLOCKS, BLOCKS), BF16),
             pltpu.VMEM((512, 256), F32),
-            chunk, chunk, chunk, chunk,
+            chunk, chunk, quarters, quarters,
             pltpu.VMEM((4, 4, 16, 2, 8, 128), F32),
             pltpu.VMEM((4, 16, 2, 8, 128), F32),
             pltpu.VMEM((2, 128, 256), BF16),
             pltpu.VMEM((32, 256, 128), BF16),
             pltpu.VMEM((32, 256, 128), BF16),
             pltpu.VMEM((2, 2, 8, 64, 128), F32),
-            eighths, eighths, eighths,
+            eighths, sixteen, sixteen,
             pltpu.VMEM((2, 64, 128), F32),
-            DMA((5,)), DMA((16,)), DMA((16,)), DMA((4, 16)), DMA((4, 16)),
+            DMA((5,)), DMA, DMA, DMA((4,)), DMA((4,)),
             DMA((2, 4)), DMA((2, 4)), DMA((4,)), DMA((4,)), DMA((4,)), DMA((4,)),
-            DMA((4,)), DMA((4,)), DMA((2, 16)), DMA((2, 2, 8)),
+            DMA((4,)), DMA((4,)), DMA, DMA,
         ],
         compiler_params=pltpu.CompilerParams(
             vmem_limit_bytes=60 * 2**20, collective_id=0, has_side_effects=True

time: 63.3 us -> 61.2 us (0.967)
  Pallas kernels: 61.6 us -> 59.5 us
    pallas_call x1, Pallas kernels: 61.6 us -> 59.5 us  [on_device(): pl.pallas_call(kernel, out_shape=jax.ShapeDtypeStruct((4, 2, 16, 128), F3...]
where the time goes in v6:
time: 61.2 us; the launch traced here: 61 us
  Pallas kernels  59.5 us (97%)
  local copies, waits for them, and re-layouts  1.47 us (2%)
    pallas_call x1, Pallas kernels, on_device(): pl.pallas_call(kernel, out_shape=jax.ShapeDtypeStruct((4, 2, 16, 128), F3...  59.5 us
    unnamed x1, local copies, waits for them, and re-layouts  1.47 us

profile of v6, /device:TPU:1, one launch (start us, length us, event | category | flops | bytes accessed | tf_op | source)
XLA Modules:
  0.0 61.0 jit_solution(2263041798535247472)
XLA Ops:
  0.0 59.5 %coherence.1 = f32[4,2,16,128]{3,2,1,0:T(8,128)} custom-call(f32[2,16,32,128]{3,2,1,0:T(8,128)} %x_hbm.1, s32[1,64]{1,0:T(1,128)} %bitcast.2, s32[1,64]{1,0:T(1,128)} %bitcast.3, bf16[2,256,256]{2,1,0:T(8,128)(2,1)} %constant.4.clone.ctable_hbm, bf16[2,1024,512]{2,1,0:T(8,128)(2,1)} %constant.5.clone.table_hbm), custom_call_target="tpu_custom_call" | custom-call | tf_op jit(solution)/shard_map/coherence/pallas_call | solution.py:368
  59.5 1.5 %copy.7 = f32[4,2,16,128]{3,2,1,0:T(8,128)} copy(f32[4,2,16,128]{3,2,1,0:T(8,128)} %coherence.1) | data formatting | bytes 131072

commit v7 on v5

v7 whole, which is shorter than its diff:
```python
import math

import jax
import jax.numpy as jnp
import ml_dtypes
import numpy as np
from jax import lax
from jax.experimental import pallas as pl
from jax.experimental.pallas import tpu as pltpu
from jax.sharding import Mesh
from jax.sharding import PartitionSpec as P

CHANNELS = 128
BLOCKS = 512
ALPHAS = 64
SHIFTS = 8
FLOOR = 0.1
F32 = jnp.float32
BF16 = jnp.bfloat16
VMEM = pl.BlockSpec(memory_space=pltpu.VMEM)
HBM = pl.BlockSpec(memory_space=pltpu.HBM)


def halves(table):
    high = table.astype(ml_dtypes.bfloat16)
    low = (table - high.astype(np.float64)).astype(ml_dtypes.bfloat16)
    return np.stack([high, low])


def channel_table():
    n = np.arange(CHANNELS)
    window = 0.5 - 0.5 * np.cos(2 * np.pi * n / CHANNELS)
    angle = 2 * np.pi * (n[:, None] * n[None, :] % CHANNELS) / CHANNELS
    cosine = window[:, None] * np.cos(angle) / math.sqrt(CHANNELS)
    sine = window[:, None] * np.sin(angle) / math.sqrt(CHANNELS)
    return halves(np.block([[cosine, -sine], [sine, cosine]]))


def half_order():
    return np.arange(BLOCKS // 2).reshape(8, 4, 8).transpose(1, 0, 2).reshape(-1)


def block_table():
    n = half_order()
    angle = 4 * np.pi * (n[:, None] * n[None, :] % (BLOCKS // 2)) / BLOCKS
    return halves(np.concatenate([np.cos(angle), np.sin(angle)], 0) / math.sqrt(BLOCKS))


def twiddles():
    angle = 2 * np.pi * half_order()[:, None] / BLOCKS * np.ones((1, 128))
    sign = np.where(np.arange(128) < 64, 1.0, -1.0)
    return np.stack([np.cos(angle), np.sin(angle) * sign]).astype(np.float32)


def split(x):
    high = x.astype(BF16)
    return high, (x - high.astype(F32)).astype(BF16)


def dot3(a, b, dims):
    def one(u, v):
        return lax.dot_general(u, v, (dims, ((), ())), preferred_element_type=F32)

    rows = a[0].shape[0]
    top = one(jnp.concatenate(a, 0), b[0])
    return top[:rows] + (top[rows:] + one(a[0], b[1]))


def lane_block(shape, width):
    return lax.broadcasted_iota(jnp.int32, shape, len(shape) - 1) // width % 2


def swap_blocks(tiles):
    tiles = list(tiles)
    for bit in (1, 2, 4, 8):
        width = 8 * bit
        upper = lane_block(tiles[0].shape, width) == 1
        for i in range(16):
            if i & bit:
                continue
            a, b = tiles[i], tiles[i | bit]
            axis = a.ndim - 1
            tiles[i] = jnp.where(upper, pltpu.roll(b, width, axis), a)
            tiles[i | bit] = jnp.where(upper, b, pltpu.roll(a, 128 - width, axis))
    return tiles


def remote(src, dst, send, recv, **where):
    return pltpu.make_async_remote_copy(
        src_ref=src,
        dst_ref=dst,
        send_sem=send,
        recv_sem=recv,
        device_id=where,
        device_id_type=pl.DeviceIdType.MESH,
    )


def phase_rows(bins_ref, offsets_ref, first):
    row = lax.broadcasted_iota(jnp.int32, (ALPHAS, ALPHAS), 0)
    same = row == lax.broadcasted_iota(jnp.int32, (ALPHAS, ALPHAS), 1)

    def column(ref):
        return jnp.sum(jnp.where(same, ref[...].astype(F32), 0.0), 1, keepdims=True)

    lane = lax.broadcasted_iota(jnp.int32, (ALPHAS, 256), 1)
    turns = column(bins_ref).astype(jnp.int32) * (first + lane // 8) % BLOCKS
    angle = turns.astype(F32) * (2.0 * math.pi / BLOCKS)
    chosen = column(offsets_ref).astype(jnp.int32) == lane % 8
    both = [jnp.where(chosen, f(angle) * (1.0 / 256.0), 0.0) for f in (jnp.cos, jnp.sin)]
    return split(jnp.concatenate(both, 0))


def kernel(
    x_hbm, bins_hbm, offsets_hbm, ctable_hbm, table_hbm, twiddle_hbm, out_ref,
    bins_ref, offsets_ref, x_ref, ctable_ref, table_ref, twiddle_ref, mid_ref, made_ref, got_ref, back_ref, land_ref,
    right_ref, other_ref, phase_ref, high_ref, low_ref, high2_ref, low2_ref, left_ref,
    part_ref, pair_ref, sum_ref, all_ref, part2_ref, pair2_ref, sum2_ref, all2_ref, res_ref, late_ref,
    load_sem, send1, recv1, send2, recv2, sendx, recvx, sendf, recvf, sendz, recvz,
    sendp, recvp, sends, recvs,
):
    chan, x, z = lax.axis_index("chan"), lax.axis_index("x"), lax.axis_index("z")
    core, place = lax.rem(chan, 2), chan // 2
    mate = chan + 1 - 2 * core
    after, before = lax.rem(x + 1, 4), lax.rem(x + 3, 4)

    loads = [
        pltpu.make_async_copy(src, dst, load_sem.at[i])
        for i, (src, dst) in enumerate(
            [
                (x_hbm, x_ref),
                (ctable_hbm, ctable_ref),
                (table_hbm, table_ref),
                (bins_hbm, bins_ref),
                (offsets_hbm, offsets_ref),
                (twiddle_hbm, twiddle_ref),
            ]
        )
    ]
    for load in loads:
        load.start()

    barrier = pltpu.get_barrier_semaphore()
    peers = [{"chan": lax.rem(chan + o, 16)} for o in range(1, 16)]
    peers += [{"x": after}, {"x": before}]
    peers += [{"z": 1 - z, "chan": lax.rem(place + o, 8) * 2 + core} for o in range(8)]
    for where in peers:
        pl.semaphore_signal(barrier, device_id=where, device_id_type=pl.DeviceIdType.MESH)

    loads[0].wait()
    loads[1].wait()
    both = jnp.concatenate([x_ref[0].reshape(512, 128), x_ref[1].reshape(512, 128)], 1)
    mid_ref[...] = dot3(split(both), (ctable_ref[0], ctable_ref[1]), ((1,), (0,)))
    def tiles_of(h):
        for mc in range(4):
            tiles = [
                mid_ref[s * 32 + mc * 8 : s * 32 + mc * 8 + 8, c * 128 : c * 128 + 128]
                for c in range(2)
                for s in range(h * 8, h * 8 + 8)
            ]
            for dest, tile in enumerate(swap_blocks(tiles)):
                made_ref[h, dest, mc] = tile

    def exchange(src, dst, send, recv, o):
        peer = lax.rem(chan + o, 16)
        return remote(src.at[peer], dst.at[chan], send, recv, chan=peer)

    def everyone(src, dst, send, recv):
        most = pl.ds(0, 15)
        return remote(src.at[most], dst.at[most], send, recv, chan=mate)

    def first(h):
        return made_ref.at[h], got_ref.at[h], send1.at[h], recv1.at[h]

    def second(h):
        return back_ref.at[h], land_ref.at[h], send2.at[h], recv2.at[h]

    def send_all(group):
        @pl.loop(1, 16)
        def _(o):
            exchange(*group, o).start()

    tiles_of(0)
    pl.semaphore_wait(barrier, len(peers))
    send_all(first(0))
    tiles_of(1)
    everyone(*first(0)).wait_send()
    send_all(first(1))
    for h in range(2):
        got_ref[h, chan] = made_ref[h, chan]
    for load in loads[2:]:
        load.wait()
    phase_ref[0], phase_ref[1] = phase_rows(bins_ref, offsets_ref, chan * 32)

    first_part = lax.broadcasted_iota(jnp.int32, (BLOCKS // 2, 256), 1) % 128 < 64

    def turned(u):
        return jnp.concatenate([pltpu.roll(u[:, i : i + 128], 64, 1) for i in (0, 128)], 1)

    def transform(v):
        u = dot3((table_ref[0], table_ref[1]), split(v), ((1,), (0,)))
        return u[:256], turned(u[256:])

    for h in range(2):
        everyone(*first(h)).wait_recv()
        low, high = (
            jnp.concatenate([got_ref[h, i : i + 8, mc].reshape(64, 128) for mc in range(4)], 0)
            for i in (0, 8)
        )
        odd = low - high
        odd = odd * twiddle_ref[0] + pltpu.roll(odd, 64, 1) * twiddle_ref[1]
        cosine, sine = transform(jnp.concatenate([low + high, odd], 1))
        spectra = cosine + jnp.where(first_part, sine, -sine)
        power = spectra * spectra
        power = power + turned(power)
        cosine, sine = transform(spectra / jnp.sqrt(power + FLOOR))
        blocks = cosine - jnp.where(first_part, sine, -sine)
        even, odd = blocks[:, :128], blocks[:, 128:]
        odd = odd * twiddle_ref[0] - pltpu.roll(odd, 64, 1) * twiddle_ref[1]
        for i, half in ((0, even + odd), (8, even - odd)):
            for mc in range(4):
                back_ref[h, i : i + 8, mc] = half[mc * 64 : mc * 64 + 64].reshape(8, 8, 128)
        send_all(second(h))
        land_ref[h, chan] = back_ref[h, chan]

    def eight(i, mc, h):
        return right_ref.at[i, mc, pl.ds(h * 8, 8)]

    def to_x(h, mc, way, incoming=False):
        peer = (after, before)[way ^ incoming]
        at = peer if incoming else x
        return remote(
            eight(x, mc, h), eight(at, mc, h), sendx.at[way, h, mc], recvx.at[way, h, mc], x=peer
        )

    def passed(h, mc, way, incoming=False):
        source, peer = (before, after) if way == 0 else (after, before)
        at = lax.rem(x + 2, 4) if incoming else source
        four = pl.ds(h * 8 + way * 4, 4)
        return remote(
            right_ref.at[source, mc, four], right_ref.at[at, mc, four],
            sendf.at[way, h, mc], recvf.at[way, h, mc], x=peer,
        )

    def to_z(h, mc):
        return remote(
            eight(x, mc, h), other_ref.at[mc, pl.ds(h * 8, 8)], sendz.at[h, mc], recvz.at[h, mc], z=1 - z
        )

    def turn(h, mc):
        tiles = swap_blocks([land_ref[h, i, mc] for i in range(16)])
        for i, tile in enumerate(tiles):
            right_ref[x, mc, h * 8 + i % 8, i // 8] = tile
        to_x(h, mc, 0).start()
        to_x(h, mc, 1).start()
        to_z(h, mc).start()

    def forward(h, mc):
        for way in range(2):
            to_x(h, mc, way, True).wait_recv()
            passed(h, mc, way).start()

    far = lax.rem(x + 2, 4)

    def shifted(mc, r):
        left = []
        for c in range(2):
            rows = []
            for a in range(32):
                if a < 16:
                    row = right_ref[x, mc, a, c, pl.ds(r, 1), :]
                else:
                    row = other_ref[mc, a - 16, c, pl.ds(r, 1), :]
                rows.append(pltpu.roll(jnp.broadcast_to(row, (8, 128)), 0, 1, stride=1, stride_axis=0))
            left.append(jnp.concatenate(rows, 0))
        return split(jnp.concatenate(left, 1))

    def facing(i, mc, r):
        tall = right_ref.at[i, mc].reshape(256, 128)
        real, imag = (tall[pl.ds(r + c * 8, 16, stride=16), :] for c in range(2))
        return [jnp.concatenate([real, imag], 1), jnp.concatenate([-imag, real], 1)]

    def product(mc, r, part):
        m = mc * 8 + r
        if part == 0:
            left = shifted(mc, r)
            left_ref[0, m], left_ref[1, m] = left
            rows = []
            for i in range(4):
                rows += facing(jnp.where(far == i, x, i), mc, r)
        else:
            left = left_ref[0, m], left_ref[1, m]
            rows = facing(far, mc, r) * 4
        out = dot3(left, split(jnp.concatenate(rows, 0)), ((1,), (1,)))
        if part == 0:
            return out.reshape(32, 8, 128)
        out = out.reshape(8, 4, 8, 128)
        group = lax.broadcasted_iota(jnp.int32, (8, 8, 128), 2) // 32
        tiles = out[:, 3]
        for i in range(3):
            tiles = jnp.where(group == i, out[:, i], tiles)
        return tiles

    def products(mc, part, high_ref, low_ref):
        def step(i, carry):
            for half in range(2):
                r = i * 4 + half * 2
                tiles = jnp.concatenate([product(mc, r, part), product(mc, r + 1, part)], 1)
                rows = pl.ds(pl.multiple_of(mc * 64 + r * 8, 16), 16)
                high_ref[:, rows, :], low_ref[:, rows, :] = split(tiles)
            return carry

        lax.fori_loop(0, 2, step, 0)

    for h in range(2):
        everyone(*second(h)).wait_recv()
        for mc in range(4):
            turn(h, mc)
    for mc in range(4):
        for h in range(2):
            forward(h, mc)
            to_z(h, mc).wait_recv()
        products(mc, 0, high_ref, low_ref)

    low_rows = lax.broadcasted_iota(jnp.int32, (8, 128), 0) < 4

    def one_pair(refs, out_ref, half, pair):
        a = half * (refs[0].shape[0] // 2) + pair * 2
        both = tuple(jnp.concatenate([ref[a], ref[a + 1]], 1) for ref in refs)
        t = dot3((phase_ref[0], phase_ref[1]), both, ((1,), (0,)))
        gs = []
        for i in range(2):
            cosine, sine = t[:64, i * 128 : i * 128 + 128], t[64:, i * 128 : i * 128 + 128]
            odd = lane_block(sine.shape, 16) == 1
            gs.append(cosine + jnp.where(odd, -pltpu.roll(sine, 16, 1), pltpu.roll(sine, 112, 1)))
        row = pl.ds(pair * 8, 8)
        for t8 in range(8):
            a0, a1 = (g[t8 * 8 : t8 * 8 + 8] for g in gs)
            out_ref[0, half, t8, row, :] = jnp.where(low_rows, a0, pltpu.roll(a1, 4, 0))
            out_ref[1, half, t8, row, :] = jnp.where(low_rows, pltpu.roll(a0, 4, 0), a1)

    def to_mate(part, half):
        return remote(
            parts[part].at[1 - core, half], pairs[part].at[half],
            sendp.at[part, half], recvp.at[part, half], chan=mate,
        )

    def last(part):
        return sums[part], alls[part], sends.at[part], recvs.at[part]

    def spread(part, o):
        peer_z, peer = lax.rem(z + o // 8, 2), lax.rem(place + lax.rem(o, 8), 8)
        src, dst, send, recv = last(part)
        return remote(
            src.at[o // 8 * 8 + peer], dst.at[z * 8 + place], send, recv,
            z=peer_z, chan=peer * 2 + core,
        )

    def add_and_send(part, half):
        to_mate(part, half).wait_recv()
        sums[part][half * 8 : half * 8 + 8] = parts[part][core, half] + pairs[part][half]

        @pl.loop(8 if half else 1, 16 if half else 8)
        def _(o):
            spread(part, o).start()

        if not half:
            alls[part][z * 8 + place] = sums[part][place]

    parts, pairs = (part_ref, part2_ref), (pair_ref, pair2_ref)
    sums, alls = (sum_ref, sum2_ref), (all_ref, all2_ref)
    for half in (1, 0):
        for pair in range(8):
            one_pair((high_ref, low_ref), part_ref, half, pair)
        to_mate(0, half).start()
    for half in (1, 0):
        add_and_send(0, half)
    for mc in range(4):
        for h in range(2):
            for way in range(2):
                passed(h, mc, way, True).wait_recv()
        products(mc, 1, high2_ref, low2_ref)
    for half in (1, 0):
        for pair in range(2):
            one_pair((high2_ref, low2_ref), part2_ref, half, pair)
        to_mate(1, half).start()
    for half in (1, 0):
        add_and_send(1, half)

    everyone(*last(0)).wait_recv()
    for h in range(2):
        res_ref[h] = jnp.sum(all_ref[h * 8 : h * 8 + 8], axis=0)
    everyone(*last(1)).wait_recv()
    for h in range(2):
        late = jnp.sum(all2_ref[h * 8 : h * 8 + 8], axis=0)
        for i in range(4):
            there = pltpu.roll(late, lax.rem(far + 4 - i, 4) * 32, 1)
            for g in range(4):
                late_ref[h, g * 16 + i * 4 : g * 16 + i * 4 + 4] = there[g * 4 : g * 4 + 4]
    missing = lax.broadcasted_iota(jnp.int32, (64, 128), 1) // 32 == far
    lo, hi = (jnp.where(missing, late_ref[h], res_ref[h]) for h in range(2))
    odd = lane_block(lo.shape, 16) == 1
    res_ref[0] = jnp.where(odd, pltpu.roll(hi, 16, 1), lo)
    res_ref[1] = jnp.where(odd, hi, pltpu.roll(lo, 112, 1))
    for j in range(4):
        for c in range(2):
            out_ref[j, c] = res_ref[c, pl.ds(j, 16, stride=4), :]

    for group in (first(1), second(0), second(1), last(0), last(1)):
        everyone(*group).wait_send()
    for mc in range(4):
        for h in range(2):
            for way in range(2):
                to_x(h, mc, way).wait_send()
                passed(h, mc, way).wait_send()
            to_z(h, mc).wait_send()
        to_mate(mc // 2, mc % 2).wait_send()


DMA = pltpu.SemaphoreType.DMA


def summed(rows):
    shapes = [(2, 2, 8), (2, 8), (16,), (16,)]
    return [pltpu.VMEM((*shape, rows, 128), F32) for shape in shapes]


def on_device(samples, bins, offsets):
    chunk = pltpu.VMEM((2, 16, 4, 8, 128), F32)
    sixteen = pltpu.VMEM((16, 64, 128), F32)
    return pl.pallas_call(
        kernel,
        out_shape=jax.ShapeDtypeStruct((4, 2, 16, 128), F32),
        in_specs=[HBM] * 6,
        out_specs=VMEM,
        scratch_shapes=[
            pltpu.VMEM((1, ALPHAS), jnp.int32),
            pltpu.VMEM((1, ALPHAS), jnp.int32),
            pltpu.VMEM((2, 16, 32, 128), F32),
            pltpu.VMEM((2, 256, 256), BF16),
            pltpu.VMEM((2, BLOCKS, BLOCKS // 2), BF16),
            pltpu.VMEM((2, BLOCKS // 2, 128), F32),
            pltpu.VMEM((512, 256), F32),
            chunk, chunk, chunk, chunk,
            pltpu.VMEM((4, 4, 16, 2, 8, 128), F32),
            pltpu.VMEM((4, 16, 2, 8, 128), F32),
            pltpu.VMEM((2, 128, 256), BF16),
            pltpu.VMEM((32, 256, 128), BF16),
            pltpu.VMEM((32, 256, 128), BF16),
            pltpu.VMEM((8, 256, 128), BF16),
            pltpu.VMEM((8, 256, 128), BF16),
            pltpu.VMEM((2, 32, 256, 256), BF16),
            *summed(64),
            *summed(16),
            pltpu.VMEM((2, 64, 128), F32),
            pltpu.VMEM((2, 64, 128), F32),
            DMA((6,)), DMA((2,)), DMA((2,)), DMA((2,)), DMA((2,)),
            DMA((2, 2, 4)), DMA((2, 2, 4)), DMA((2, 2, 4)), DMA((2, 2, 4)), DMA((2, 4)), DMA((2, 4)),
            DMA((2, 2)), DMA((2, 2)), DMA((2,)), DMA((2,)),
        ],
        compiler_params=pltpu.CompilerParams(
            vmem_limit_bytes=60 * 2**20, collective_id=0, has_side_effects=True
        ),
        name="coherence",
    )(samples, bins.reshape(1, -1), offsets.reshape(1, -1), channel_table(), block_table(), twiddles())


def solution(mesh):
    finer = Mesh(mesh.devices.reshape(4, 2, mesh.shape["chan"]), ("x", "z", "chan"))
    sensor = ("x", "z")
    return jax.shard_map(
        on_device,
        mesh=finer,
        in_specs=(P(None, sensor, "chan", None), P(), P()),
        out_specs=P("chan", None, sensor, None),
        check_vma=False,
    )
```

time: 65 us -> 55 us (0.85)
  Pallas kernels: 63.3 us -> 53.2 us
    pallas_call x1, Pallas kernels: 63.3 us -> 53.2 us  [on_device(): pl.pallas_call(kernel, out_shape=jax.ShapeDtypeStruct((4, 2, 16, 128), F3...]
where the time goes in v7:
time: 55 us; the launch traced here: 54.6 us
  Pallas kernels  53.2 us (97%)
  local copies, waits for them, and re-layouts  1.47 us (3%)
    pallas_call x1, Pallas kernels, on_device(): pl.pallas_call(kernel, out_shape=jax.ShapeDtypeStruct((4, 2, 16, 128), F3...  53.2 us
    unnamed x1, local copies, waits for them, and re-layouts  1.47 us

profile of v7, /device:TPU:1, one launch (start us, length us, event | category | flops | bytes accessed | tf_op | source)
XLA Modules:
  0.0 54.6 jit_solution(16760530748078681285)
XLA Ops:
  0.0 53.2 %coherence.1 = f32[4,2,16,128]{3,2,1,0:T(8,128)} custom-call(f32[2,16,32,128]{3,2,1,0:T(8,128)} %x_hbm.1, s32[1,64]{1,0:T(1,128)} %bitcast.2, s32[1,64]{1,0:T(1,128)} %bitcast.3, bf16[2,256,256]{2,1,0:T(8,128)(2,1)} %constant.6.clone.ctable_hbm, bf16[2,512,256]{2,1,0:T(8,128)(2,1)} %constant.7.clone.table_hbm, f32[2,256,128]{2,1,0:T(8,128)} %constant.8.clone.twiddle_hbm), custom_call_target="tpu_custom_call" | custom-call | tf_op jit(solution)/shard_map/coherence/pallas_call | solution.py:431
  53.2 1.5 %copy.8 = f32[4,2,16,128]{3,2,1,0:T(8,128)} copy(f32[4,2,16,128]{3,2,1,0:T(8,128)} %coherence.1) | data formatting | bytes 131072

commit v8 on v7

--- a/solution.py
+++ b/solution.py
@@ -96,6 +96,20 @@
     )
 
 
+def ring(d):
+    return min(d, 4 - d)
+
+
+OWNERS = sorted(
+    ((d, y, c) for d in range(2) for y in range(4) for c in range(2) if d + y + c),
+    key=lambda step: -(2 * step[0] + ring(step[1])),
+)
+PLANE = sorted(
+    ((d, y, lo) for d in range(2) for y in range(4) for lo in range(2) if d + y + lo),
+    key=lambda step: -(ring(2 * step[0] + step[2]) + ring(step[1])),
+)
+
+
 def phase_rows(bins_ref, offsets_ref, first):
     row = lax.broadcasted_iota(jnp.int32, (ALPHAS, ALPHAS), 0)
     same = row == lax.broadcasted_iota(jnp.int32, (ALPHAS, ALPHAS), 1)
@@ -143,7 +157,7 @@
     barrier = pltpu.get_barrier_semaphore()
     peers = [{"chan": lax.rem(chan + o, 16)} for o in range(1, 16)]
     peers += [{"x": after}, {"x": before}]
-    peers += [{"z": 1 - z, "chan": lax.rem(place + o, 8) * 2 + core} for o in range(8)]
+    peers += [{"z": 1 - z}]
     for where in peers:
         pl.semaphore_signal(barrier, device_id=where, device_id_type=pl.DeviceIdType.MESH)
 
@@ -161,8 +175,11 @@
             for dest, tile in enumerate(swap_blocks(tiles)):
                 made_ref[h, dest, mc] = tile
 
-    def exchange(src, dst, send, recv, o):
-        peer = lax.rem(chan + o, 16)
+    def owner(d, y, c):
+        return lax.rem(place + d * 4, 8) // 4 * 8 + lax.rem(lax.rem(place, 4) + y, 4) * 2 + (core + c) % 2
+
+    def exchange(src, dst, send, recv, step):
+        peer = owner(*step)
         return remote(src.at[peer], dst.at[chan], send, recv, chan=peer)
 
     def everyone(src, dst, send, recv):
@@ -176,9 +193,8 @@
         return back_ref.at[h], land_ref.at[h], send2.at[h], recv2.at[h]
 
     def send_all(group):
-        @pl.loop(1, 16)
-        def _(o):
-            exchange(*group, o).start()
+        for step in OWNERS:
+            exchange(*group, step).start()
 
     tiles_of(0)
     pl.semaphore_wait(barrier, len(peers))
@@ -316,7 +332,8 @@
         everyone(*second(h)).wait_recv()
         for mc in range(4):
             turn(h, mc)
-    for mc in range(4):
+    @pl.loop(0, 4)
+    def _(mc):
         for h in range(2):
             forward(h, mc)
             to_z(h, mc).wait_recv()
@@ -348,11 +365,11 @@
     def last(part):
         return sums[part], alls[part], sends.at[part], recvs.at[part]
 
-    def spread(part, o):
-        peer_z, peer = lax.rem(z + o // 8, 2), lax.rem(place + lax.rem(o, 8), 8)
+    def spread(part, d, y, lo):
+        peer_z, peer = (z + lo) % 2, owner(d, y, 0) // 2
         src, dst, send, recv = last(part)
         return remote(
-            src.at[o // 8 * 8 + peer], dst.at[z * 8 + place], send, recv,
+            src.at[lo * 8 + peer], dst.at[z * 8 + place], send, recv,
             z=peer_z, chan=peer * 2 + core,
         )
 
@@ -360,9 +377,9 @@
         to_mate(part, half).wait_recv()
         sums[part][half * 8 : half * 8 + 8] = parts[part][core, half] + pairs[part][half]
 
-        @pl.loop(8 if half else 1, 16 if half else 8)
-        def _(o):
-            spread(part, o).start()
+        for step in PLANE:
+            if step[2] == half:
+                spread(part, *step).start()
 
         if not half:
             alls[part][z * 8 + place] = sums[part][place]
@@ -375,7 +392,8 @@
         to_mate(0, half).start()
     for half in (1, 0):
         add_and_send(0, half)
-    for mc in range(4):
+    @pl.loop(0, 4)
+    def _(mc):
         for h in range(2):
             for way in range(2):
                 passed(h, mc, way, True).wait_recv()
@@ -387,6 +405,15 @@
     for half in (1, 0):
         add_and_send(1, half)
 
+    for group in (first(1), second(0), second(1), last(0)):
+        everyone(*group).wait_send()
+    for mc in range(4):
+        for h in range(2):
+            for way in range(2):
+                to_x(h, mc, way).wait_send()
+                passed(h, mc, way).wait_send()
+            to_z(h, mc).wait_send()
+        to_mate(mc // 2, mc % 2).wait_send()
     everyone(*last(0)).wait_recv()
     for h in range(2):
         res_ref[h] = jnp.sum(all_ref[h * 8 : h * 8 + 8], axis=0)
@@ -406,15 +433,7 @@
         for c in range(2):
             out_ref[j, c] = res_ref[c, pl.ds(j, 16, stride=4), :]
 
-    for group in (first(1), second(0), second(1), last(0), last(1)):
-        everyone(*group).wait_send()
-    for mc in range(4):
-        for h in range(2):
-            for way in range(2):
-                to_x(h, mc, way).wait_send()
-                passed(h, mc, way).wait_send()
-            to_z(h, mc).wait_send()
-        to_mate(mc // 2, mc % 2).wait_send()
+    everyone(*last(1)).wait_send()
 
 
 DMA = pltpu.SemaphoreType.DMA

time: 55 us -> 53.5 us (0.973)
  Pallas kernels: 53.2 us -> 51.6 us
    pallas_call x1, Pallas kernels: 53.2 us -> 51.6 us  [on_device(): pl.pallas_call(kernel, out_shape=jax.ShapeDtypeStruct((4, 2, 16, 128), F3...]
where the time goes in v8:
time: 53.5 us; the launch traced here: 53 us
  Pallas kernels  51.6 us (96%)
  local copies, waits for them, and re-layouts  1.47 us (3%)
    pallas_call x1, Pallas kernels, on_device(): pl.pallas_call(kernel, out_shape=jax.ShapeDtypeStruct((4, 2, 16, 128), F3...  51.6 us
    unnamed x1, local copies, waits for them, and re-layouts  1.47 us

profile of v8, /device:TPU:1, one launch (start us, length us, event | category | flops | bytes accessed | tf_op | source)
XLA Modules:
  0.0 53.0 jit_solution(10345480450174705594)
XLA Ops:
  0.0 51.6 %coherence.1 = f32[4,2,16,128]{3,2,1,0:T(8,128)} custom-call(f32[2,16,32,128]{3,2,1,0:T(8,128)} %x_hbm.1, s32[1,64]{1,0:T(1,128)} %bitcast.2, s32[1,64]{1,0:T(1,128)} %bitcast.3, bf16[2,256,256]{2,1,0:T(8,128)(2,1)} %constant.6.clone.ctable_hbm, bf16[2,512,256]{2,1,0:T(8,128)(2,1)} %constant.7.clone.table_hbm, f32[2,256,128]{2,1,0:T(8,128)} %constant.8.clone.twiddle_hbm), custom_call_target="tpu_custom_call" | custom-call | tf_op jit(solution)/shard_map/coherence/pallas_call | solution.py:450
  51.6 1.5 %copy.8 = f32[4,2,16,128]{3,2,1,0:T(8,128)} copy(f32[4,2,16,128]{3,2,1,0:T(8,128)} %coherence.1) | data formatting | bytes 131072

commit v9 on v8

--- a/solution.py
+++ b/solution.py
@@ -189,8 +189,8 @@
     def first(h):
         return made_ref.at[h], got_ref.at[h], send1.at[h], recv1.at[h]
 
-    def second(h):
-        return back_ref.at[h], land_ref.at[h], send2.at[h], recv2.at[h]
+    def second(h, part):
+        return back_ref.at[h, part], land_ref.at[h, part], send2.at[h, part], recv2.at[h, part]
 
     def send_all(group):
         for step in OWNERS:
@@ -219,6 +219,9 @@
 
     for h in range(2):
         everyone(*first(h)).wait_recv()
+        if h:
+            everyone(*second(0, 0)).wait_send()
+            send_all(second(0, 1))
         low, high = (
             jnp.concatenate([got_ref[h, i : i + 8, mc].reshape(64, 128) for mc in range(4)], 0)
             for i in (0, 8)
@@ -235,9 +238,13 @@
         odd = odd * twiddle_ref[0] - pltpu.roll(odd, 64, 1) * twiddle_ref[1]
         for i, half in ((0, even + odd), (8, even - odd)):
             for mc in range(4):
-                back_ref[h, i : i + 8, mc] = half[mc * 64 : mc * 64 + 64].reshape(8, 8, 128)
-        send_all(second(h))
-        land_ref[h, chan] = back_ref[h, chan]
+                rows = half[mc * 64 : mc * 64 + 64].reshape(8, 8, 128)
+                back_ref[h, mc // 2, i : i + 8, mc % 2] = rows
+        for part in range(2):
+            land_ref[h, part, chan] = back_ref[h, part, chan]
+        send_all(second(h, 0))
+        if h:
+            send_all(second(1, 1))
 
     def eight(i, mc, h):
         return right_ref.at[i, mc, pl.ds(h * 8, 8)]
@@ -264,7 +271,7 @@
         )
 
     def turn(h, mc):
-        tiles = swap_blocks([land_ref[h, i, mc] for i in range(16)])
+        tiles = swap_blocks([land_ref[h, mc // 2, i, mc % 2] for i in range(16)])
         for i, tile in enumerate(tiles):
             right_ref[x, mc, h * 8 + i % 8, i // 8] = tile
         to_x(h, mc, 0).start()
@@ -306,8 +313,11 @@
                 rows += facing(jnp.where(far == i, x, i), mc, r)
         else:
             left = left_ref[0, m], left_ref[1, m]
-            rows = facing(far, mc, r) * 4
-        out = dot3(left, split(jnp.concatenate(rows, 0)), ((1,), (1,)))
+            rows = facing(far, mc, r)
+        right = split(jnp.concatenate(rows, 0))
+        if part:
+            right = [jnp.concatenate([half] * 4, 0) for half in right]
+        out = dot3(left, right, ((1,), (1,)))
         if part == 0:
             return out.reshape(32, 8, 128)
         out = out.reshape(8, 4, 8, 128)
@@ -329,8 +339,9 @@
         lax.fori_loop(0, 2, step, 0)
 
     for h in range(2):
-        everyone(*second(h)).wait_recv()
         for mc in range(4):
+            if mc % 2 == 0:
+                everyone(*second(h, mc // 2)).wait_recv()
             turn(h, mc)
     @pl.loop(0, 4)
     def _(mc):
@@ -390,14 +401,23 @@
         for pair in range(8):
             one_pair((high_ref, low_ref), part_ref, half, pair)
         to_mate(0, half).start()
-    for half in (1, 0):
-        add_and_send(0, half)
-    @pl.loop(0, 4)
-    def _(mc):
+    def late_products(mc):
         for h in range(2):
             for way in range(2):
                 passed(h, mc, way, True).wait_recv()
         products(mc, 1, high2_ref, low2_ref)
+
+    @pl.loop(0, 1)
+    def _(mc):
+        late_products(mc)
+
+    for half in (1, 0):
+        add_and_send(0, half)
+
+    @pl.loop(1, 4)
+    def _(mc):
+        late_products(mc)
+
     for half in (1, 0):
         for pair in range(2):
             one_pair((high2_ref, low2_ref), part2_ref, half, pair)
@@ -405,7 +425,7 @@
     for half in (1, 0):
         add_and_send(1, half)
 
-    for group in (first(1), second(0), second(1), last(0)):
+    for group in (first(1), second(0, 1), second(1, 0), second(1, 1), last(0)):
         everyone(*group).wait_send()
     for mc in range(4):
         for h in range(2):
@@ -446,6 +466,7 @@
 
 def on_device(samples, bins, offsets):
     chunk = pltpu.VMEM((2, 16, 4, 8, 128), F32)
+    pieces = pltpu.VMEM((2, 2, 16, 2, 8, 128), F32)
     sixteen = pltpu.VMEM((16, 64, 128), F32)
     return pl.pallas_call(
         kernel,
@@ -460,7 +481,7 @@
             pltpu.VMEM((2, BLOCKS, BLOCKS // 2), BF16),
             pltpu.VMEM((2, BLOCKS // 2, 128), F32),
             pltpu.VMEM((512, 256), F32),
-            chunk, chunk, chunk, chunk,
+            chunk, chunk, pieces, pieces,
             pltpu.VMEM((4, 4, 16, 2, 8, 128), F32),
             pltpu.VMEM((4, 16, 2, 8, 128), F32),
             pltpu.VMEM((2, 128, 256), BF16),
@@ -473,7 +494,7 @@
             *summed(16),
             pltpu.VMEM((2, 64, 128), F32),
             pltpu.VMEM((2, 64, 128), F32),
-            DMA((6,)), DMA((2,)), DMA((2,)), DMA((2,)), DMA((2,)),
+            DMA((6,)), DMA((2,)), DMA((2,)), DMA((2, 2)), DMA((2, 2)),
             DMA((2, 2, 4)), DMA((2, 2, 4)), DMA((2, 2, 4)), DMA((2, 2, 4)), DMA((2, 4)), DMA((2, 4)),
             DMA((2, 2)), DMA((2, 2)), DMA((2,)), DMA((2,)),
         ],

time: 53.5 us -> 52.6 us (0.983)
  Pallas kernels: 51.6 us -> 50.9 us
    pallas_call x1, Pallas kernels: 51.6 us -> 50.9 us  [on_device(): pl.pallas_call(kernel, out_shape=jax.ShapeDtypeStruct((4, 2, 16, 128), F3...]
where the time goes in v9:
time: 52.6 us; the launch traced here: 52.4 us
  Pallas kernels  50.9 us (97%)
  local copies, waits for them, and re-layouts  1.47 us (3%)
    pallas_call x1, Pallas kernels, on_device(): pl.pallas_call(kernel, out_shape=jax.ShapeDtypeStruct((4, 2, 16, 128), F3...  50.9 us
    unnamed x1, local copies, waits for them, and re-layouts  1.47 us

profile of v9, /device:TPU:1, one launch (start us, length us, event | category | flops | bytes accessed | tf_op | source)
XLA Modules:
  0.0 52.4 jit_solution(16898799612088458208)
XLA Ops:
  0.0 50.9 %coherence.1 = f32[4,2,16,128]{3,2,1,0:T(8,128)} custom-call(f32[2,16,32,128]{3,2,1,0:T(8,128)} %x_hbm.1, s32[1,64]{1,0:T(1,128)} %bitcast.2, s32[1,64]{1,0:T(1,128)} %bitcast.3, bf16[2,256,256]{2,1,0:T(8,128)(2,1)} %constant.6.clone.ctable_hbm, bf16[2,512,256]{2,1,0:T(8,128)(2,1)} %constant.7.clone.table_hbm, f32[2,256,128]{2,1,0:T(8,128)} %constant.8.clone.twiddle_hbm), custom_call_target="tpu_custom_call" | custom-call | tf_op jit(solution)/shard_map/coherence/pallas_call | solution.py:471
  50.9 1.5 %copy.8 = f32[4,2,16,128]{3,2,1,0:T(8,128)} copy(f32[4,2,16,128]{3,2,1,0:T(8,128)} %coherence.1) | data formatting | bytes 131072

commit v10 on v9

--- a/solution.py
+++ b/solution.py
@@ -468,6 +468,10 @@
     chunk = pltpu.VMEM((2, 16, 4, 8, 128), F32)
     pieces = pltpu.VMEM((2, 2, 16, 2, 8, 128), F32)
     sixteen = pltpu.VMEM((16, 64, 128), F32)
+    given = [
+        samples, bins.reshape(1, -1), offsets.reshape(1, -1),
+        jnp.asarray(channel_table()), jnp.asarray(block_table()), jnp.asarray(twiddles()),
+    ]
     return pl.pallas_call(
         kernel,
         out_shape=jax.ShapeDtypeStruct((4, 2, 16, 128), F32),
@@ -499,10 +503,10 @@
             DMA((2, 2)), DMA((2, 2)), DMA((2,)), DMA((2,)),
         ],
         compiler_params=pltpu.CompilerParams(
-            vmem_limit_bytes=60 * 2**20, collective_id=0, has_side_effects=True
+            vmem_limit_bytes=40 * 2**20, collective_id=0, has_side_effects=True
         ),
         name="coherence",
-    )(samples, bins.reshape(1, -1), offsets.reshape(1, -1), channel_table(), block_table(), twiddles())
+    )(*(pltpu.with_memory_space_constraint(v, pltpu.HBM) for v in given))
 
 
 def solution(mesh):

time: 52.6 us -> 51 us (0.970)
  local copies, waits for them, and re-layouts: 1.47 us -> 0.63 us
  Pallas kernels: 50.9 us -> 50.3 us
    unnamed x1, local copies, waits for them, and re-layouts: 1.47 us -> 0.63 us
    pallas_call x1, Pallas kernels: 50.9 us -> 50.3 us  [on_device(): pl.pallas_call(kernel, out_shape=jax.ShapeDtypeStruct((4, 2, 16, 128), F3...]
where the time goes in v10:
time: 51 us; the launch traced here: 50.9 us
  Pallas kernels  50.3 us (99%)
  local copies, waits for them, and re-layouts  0.63 us (1%)
    pallas_call x1, Pallas kernels, on_device(): pl.pallas_call(kernel, out_shape=jax.ShapeDtypeStruct((4, 2, 16, 128), F3...  50.3 us

profile of v10, /device:TPU:1, one launch (start us, length us, event | category | flops | bytes accessed | tf_op | source)
XLA Modules:
  0.0 50.9 jit_solution(867654061754081068)
XLA Ops:
  0.0 50.3 %coherence.1 = f32[4,2,16,128]{3,2,1,0:T(8,128)S(1)} custom-call(f32[2,16,32,128]{3,2,1,0:T(8,128)} %x_hbm.1, s32[1,64]{1,0:T(1,128)} %bitcast.2, s32[1,64]{1,0:T(1,128)} %bitcast.3, bf16[2,256,256]{2,1,0:T(8,128)(2,1)} %constant.6.clone.ctable_hbm, bf16[2,512,256]{2,1,0:T(8,128)(2,1)} %constant.7.clone.table_hbm, f32[2,256,128]{2,1,0:T(8,128)} %constant.8.clone.twiddle_hbm), custom_call_target="tpu_custom_call" | custom-call | tf_op jit(solution)/shard_map/coherence/pallas_call | solution.py:475
  50.3 0.6 %copy.8 = f32[4,2,16,128]{3,2,1,0:T(8,128)} copy(f32[4,2,16,128]{3,2,1,0:T(8,128)S(1)} %coherence.1) | data formatting | bytes 131072

commit v11 on v10

--- a/solution.py
+++ b/solution.py
@@ -249,25 +249,23 @@
     def eight(i, mc, h):
         return right_ref.at[i, mc, pl.ds(h * 8, 8)]
 
-    def to_x(h, mc, way, incoming=False):
-        peer = (after, before)[way ^ incoming]
-        at = peer if incoming else x
+    def to_x(h, mc, way):
+        peer = (after, before)[way]
         return remote(
-            eight(x, mc, h), eight(at, mc, h), sendx.at[way, h, mc], recvx.at[way, h, mc], x=peer
-        )
-
-    def passed(h, mc, way, incoming=False):
+            eight(x, mc, h), eight(x, mc, h), sendx, recvx.at[h, mc], x=peer
+        )
+
+    def passed(h, mc, way):
         source, peer = (before, after) if way == 0 else (after, before)
-        at = lax.rem(x + 2, 4) if incoming else source
         four = pl.ds(h * 8 + way * 4, 4)
         return remote(
-            right_ref.at[source, mc, four], right_ref.at[at, mc, four],
-            sendf.at[way, h, mc], recvf.at[way, h, mc], x=peer,
+            right_ref.at[source, mc, four], right_ref.at[source, mc, four],
+            sendf, recvf.at[mc], x=peer,
         )
 
     def to_z(h, mc):
         return remote(
-            eight(x, mc, h), other_ref.at[mc, pl.ds(h * 8, 8)], sendz.at[h, mc], recvz.at[h, mc], z=1 - z
+            eight(x, mc, h), other_ref.at[mc, pl.ds(h * 8, 8)], sendz, recvz.at[mc], z=1 - z
         )
 
     def turn(h, mc):
@@ -278,9 +276,13 @@
         to_x(h, mc, 1).start()
         to_z(h, mc).start()
 
+    def whole(count, send, recv):
+        some = right_ref.at[0, pl.ds(0, count)] if count <= 4 else right_ref.at[pl.ds(0, count // 4)]
+        return remote(some, some, send, recv, x=after)
+
     def forward(h, mc):
+        whole(1, sendx, recvx.at[h, mc]).wait_recv()
         for way in range(2):
-            to_x(h, mc, way, True).wait_recv()
             passed(h, mc, way).start()
 
     far = lax.rem(x + 2, 4)
@@ -347,7 +349,7 @@
     def _(mc):
         for h in range(2):
             forward(h, mc)
-            to_z(h, mc).wait_recv()
+        whole(1, sendz, recvz.at[mc]).wait_recv()
         products(mc, 0, high_ref, low_ref)
 
     low_rows = lax.broadcasted_iota(jnp.int32, (8, 128), 0) < 4
@@ -402,9 +404,7 @@
             one_pair((high_ref, low_ref), part_ref, half, pair)
         to_mate(0, half).start()
     def late_products(mc):
-        for h in range(2):
-            for way in range(2):
-                passed(h, mc, way, True).wait_recv()
+        whole(1, sendf, recvf.at[mc]).wait_recv()
         products(mc, 1, high2_ref, low2_ref)
 
     @pl.loop(0, 1)
@@ -427,13 +427,12 @@
 
     for group in (first(1), second(0, 1), second(1, 0), second(1, 1), last(0)):
         everyone(*group).wait_send()
-    for mc in range(4):
-        for h in range(2):
-            for way in range(2):
-                to_x(h, mc, way).wait_send()
-                passed(h, mc, way).wait_send()
-            to_z(h, mc).wait_send()
-        to_mate(mc // 2, mc % 2).wait_send()
+    whole(8, sendx, recvx.at[0, 0]).wait_send()
+    whole(4, sendf, recvf.at[0]).wait_send()
+    whole(4, sendz, recvz.at[0]).wait_send()
+    for part in range(2):
+        for half in range(2):
+            to_mate(part, half).wait_send()
     everyone(*last(0)).wait_recv()
     for h in range(2):
         res_ref[h] = jnp.sum(all_ref[h * 8 : h * 8 + 8], axis=0)
@@ -499,7 +498,7 @@
             pltpu.VMEM((2, 64, 128), F32),
             pltpu.VMEM((2, 64, 128), F32),
             DMA((6,)), DMA((2,)), DMA((2,)), DMA((2, 2)), DMA((2, 2)),
-            DMA((2, 2, 4)), DMA((2, 2, 4)), DMA((2, 2, 4)), DMA((2, 2, 4)), DMA((2, 4)), DMA((2, 4)),
+            DMA, DMA((2, 4)), DMA, DMA((4,)), DMA, DMA((4,)),
             DMA((2, 2)), DMA((2, 2)), DMA((2,)), DMA((2,)),
         ],
         compiler_params=pltpu.CompilerParams(

time: 51 us -> 50.5 us (level)
  Pallas kernels: 50.3 us -> 49.7 us
    pallas_call x1, Pallas kernels: 50.3 us -> 49.7 us  [on_device(): pl.pallas_call(kernel, out_shape=jax.ShapeDtypeStruct((4, 2, 16, 128), F3...]
where the time goes in v11:
time: 50.5 us; the launch traced here: 50.4 us
  Pallas kernels  49.7 us (98%)
  local copies, waits for them, and re-layouts  0.63 us (1%)
    pallas_call x1, Pallas kernels, on_device(): pl.pallas_call(kernel, out_shape=jax.ShapeDtypeStruct((4, 2, 16, 128), F3...  49.7 us

profile of v11, /device:TPU:1, one launch (start us, length us, event | category | flops | bytes accessed | tf_op | source)
XLA Modules:
  0.0 50.4 jit_solution(8314752968875742319)
XLA Ops:
  0.0 49.7 %coherence.1 = f32[4,2,16,128]{3,2,1,0:T(8,128)S(1)} custom-call(f32[2,16,32,128]{3,2,1,0:T(8,128)} %x_hbm.1, s32[1,64]{1,0:T(1,128)} %bitcast.2, s32[1,64]{1,0:T(1,128)} %bitcast.3, bf16[2,256,256]{2,1,0:T(8,128)(2,1)} %constant.6.clone.ctable_hbm, bf16[2,512,256]{2,1,0:T(8,128)(2,1)} %constant.7.clone.table_hbm, f32[2,256,128]{2,1,0:T(8,128)} %constant.8.clone.twiddle_hbm), custom_call_target="tpu_custom_call" | custom-call | tf_op jit(solution)/shard_map/coherence/pallas_call | solution.py:474
  49.7 0.6 %copy.8 = f32[4,2,16,128]{3,2,1,0:T(8,128)} copy(f32[4,2,16,128]{3,2,1,0:T(8,128)S(1)} %coherence.1) | data formatting | bytes 131072

commit v12 on v11

--- a/solution.py
+++ b/solution.py
@@ -155,7 +155,10 @@
         load.start()
 
     barrier = pltpu.get_barrier_semaphore()
-    peers = [{"chan": lax.rem(chan + o, 16)} for o in range(1, 16)]
+    def owner(d, y, c):
+        return lax.rem(place + d * 4, 8) // 4 * 8 + lax.rem(lax.rem(place, 4) + y, 4) * 2 + (core + c) % 2
+
+    peers = [{"chan": owner(*step)} for step in OWNERS]
     peers += [{"x": after}, {"x": before}]
     peers += [{"z": 1 - z}]
     for where in peers:
@@ -163,8 +166,13 @@
 
     loads[0].wait()
     loads[1].wait()
-    both = jnp.concatenate([x_ref[0].reshape(512, 128), x_ref[1].reshape(512, 128)], 1)
-    mid_ref[...] = dot3(split(both), (ctable_ref[0], ctable_ref[1]), ((1,), (0,)))
+    def demodulate(h):
+        both = jnp.concatenate(
+            [x_ref[c, h * 8 : h * 8 + 8].reshape(256, 128) for c in range(2)], 1
+        )
+        table = (ctable_ref[0], ctable_ref[1])
+        mid_ref[h * 256 : h * 256 + 256] = dot3(split(both), table, ((1,), (0,)))
+
     def tiles_of(h):
         for mc in range(4):
             tiles = [
@@ -175,9 +183,6 @@
             for dest, tile in enumerate(swap_blocks(tiles)):
                 made_ref[h, dest, mc] = tile
 
-    def owner(d, y, c):
-        return lax.rem(place + d * 4, 8) // 4 * 8 + lax.rem(lax.rem(place, 4) + y, 4) * 2 + (core + c) % 2
-
     def exchange(src, dst, send, recv, step):
         peer = owner(*step)
         return remote(src.at[peer], dst.at[chan], send, recv, chan=peer)
@@ -196,9 +201,11 @@
         for step in OWNERS:
             exchange(*group, step).start()
 
+    demodulate(0)
     tiles_of(0)
     pl.semaphore_wait(barrier, len(peers))
     send_all(first(0))
+    demodulate(1)
     tiles_of(1)
     everyone(*first(0)).wait_send()
     send_all(first(1))
@@ -399,7 +406,7 @@
 
     parts, pairs = (part_ref, part2_ref), (pair_ref, pair2_ref)
     sums, alls = (sum_ref, sum2_ref), (all_ref, all2_ref)
-    for half in (1, 0):
+    for half in range(2):
         for pair in range(8):
             one_pair((high_ref, low_ref), part_ref, half, pair)
         to_mate(0, half).start()
@@ -411,18 +418,18 @@
     def _(mc):
         late_products(mc)
 
-    for half in (1, 0):
+    for half in range(2):
         add_and_send(0, half)
 
     @pl.loop(1, 4)
     def _(mc):
         late_products(mc)
 
-    for half in (1, 0):
+    for half in range(2):
         for pair in range(2):
             one_pair((high2_ref, low2_ref), part2_ref, half, pair)
         to_mate(1, half).start()
-    for half in (1, 0):
+    for half in range(2):
         add_and_send(1, half)
 
     for group in (first(1), second(0, 1), second(1, 0), second(1, 1), last(0)):

time: 50.5 us -> 50.2 us (level)
  no operation moved by 1% of the time
where the time goes in v12:
time: 50.2 us; the launch traced here: 50.1 us
  Pallas kernels  49.4 us (98%)
  local copies, waits for them, and re-layouts  0.63 us (1%)
    pallas_call x1, Pallas kernels, on_device(): pl.pallas_call(kernel, out_shape=jax.ShapeDtypeStruct((4, 2, 16, 128), F3...  49.4 us

profile of v12, /device:TPU:1, one launch (start us, length us, event | category | flops | bytes accessed | tf_op | source)
XLA Modules:
  0.0 50.1 jit_solution(8235421112263981542)
XLA Ops:
  0.0 49.4 %coherence.1 = f32[4,2,16,128]{3,2,1,0:T(8,128)S(1)} custom-call(f32[2,16,32,128]{3,2,1,0:T(8,128)} %x_hbm.1, s32[1,64]{1,0:T(1,128)} %bitcast.2, s32[1,64]{1,0:T(1,128)} %bitcast.3, bf16[2,256,256]{2,1,0:T(8,128)(2,1)} %constant.6.clone.ctable_hbm, bf16[2,512,256]{2,1,0:T(8,128)(2,1)} %constant.7.clone.table_hbm, f32[2,256,128]{2,1,0:T(8,128)} %constant.8.clone.twiddle_hbm), custom_call_target="tpu_custom_call" | custom-call | tf_op jit(solution)/shard_map/coherence/pallas_call | solution.py:481
  49.4 0.6 %copy.8 = f32[4,2,16,128]{3,2,1,0:T(8,128)} copy(f32[4,2,16,128]{3,2,1,0:T(8,128)S(1)} %coherence.1) | data formatting | bytes 131072
